TPU v7x, 512 devices: a whole 4x8x8 slice. The times are simulated.
512 devices in a mesh: lat: 16 (over y_hi, z), lon: 32 (over x, y_lo, core).
Axes of the slice: x: 4, y: 8 (y_hi: 2, y_lo: 4; y = y_hi * 4 + y_lo), z: 8, core: 2. Of those that a mesh axis runs over, the one named last changes fastest.
Arguments:
- fields: float32 [1024, 1024, 256], P('lat', 'lon'), may hold values from -6 to 6
- land_sea: int32 [512, 512], P('lat', 'lon'), may hold values 0 or 1
- w_depth: float32 [3, 3, 256], replicated, may hold values from -2 to 2
- b_depth: float32 [256], replicated, may hold values from -3 to 3
- w_one: bfloat16 [3, 3, 256, 300], replicated, may hold values from -0.125 to 0.125
- b_one: float32 [300], replicated, may hold values from -3 to 3
- w_two: bfloat16 [3, 3, 300, 300], replicated, may hold values from -0.125 to 0.125
- b_two: float32 [300], replicated, may hold values from -3 to 3
Outputs:
- level_out: float32 [512, 512, 300], P('lat', 'lon')
All inputs are finite; a program needn't handle non-finite values. No bound on the sum of `land_sea` on one device may be relied on, other than what follows from the above.
Results may differ from a plain program's by a relative error of at most 0.0035.
Values may be sent and summed in bfloat16 or wider, within the bound.
No kernel may reach another device: no remote copies, remote signals or barrier semaphores. Data moves between devices by JAX's collectives and lax.ppermute only.
A program may use at most 64 MiB of HBM per device.

v0:
```python
import jax
import jax.numpy as jnp
from jax import lax
from jax.sharding import PartitionSpec as P


def shifted(block, axis, distance):
    devices = range(lax.axis_size(axis))
    route = [(i - distance, i) for i in devices if i - distance in devices]
    return lax.ppermute(block, axis, route)


def from_behind(array, axis, by):
    devices = lax.axis_size(axis)
    return lax.ppermute(array, axis, [(i, (i + by) % devices) for i in range(devices)])


def padded(cells, sides, width):
    for axis, dim in sides:
        count = lax.axis_size(axis)
        head = lax.slice_in_dim(cells, 0, width, axis=dim)
        tail = lax.slice_in_dim(cells, cells.shape[dim] - width, cells.shape[dim], axis=dim)
        cells = jnp.concatenate(
            [
                lax.ppermute(tail, axis, [(i, (i + 1) % count) for i in range(count)]),
                cells,
                lax.ppermute(head, axis, [((i + 1) % count, i) for i in range(count)]),
            ],
            axis=dim,
        )
    return cells


def clear_poles(ext, width, band_rows):
    total_rows = lax.axis_size("lat") * band_rows
    row_index = (
        lax.axis_index("lat") * band_rows + jnp.arange(ext.shape[0], dtype=jnp.int32) - width
    )
    keeping = (row_index >= 0) & (row_index < total_rows)
    return jnp.where(keeping[:, None, None], ext, jnp.zeros_like(ext))


def dilated(ext, kernel, bias, reach, rows, cols):
    out_ch = kernel.shape[3]
    total = jnp.zeros((rows, cols, out_ch), jnp.float32) + bias
    for a in range(3):
        band = ext[a * reach : a * reach + rows]
        taps = jnp.concatenate([kernel[a, 0], kernel[a, 1], kernel[a, 2]], axis=1)
        product = jnp.einsum("ijc,cd->ijd", band, taps, preferred_element_type=jnp.float32)
        for b in range(3):
            total = total + product[:, b * reach : b * reach + cols, b * out_ch : (b + 1) * out_ch]
    return total


def on_device(fields, land_sea, w_depth, b_depth, w_one, b_one, w_two, b_two):
    rows = land_sea.shape[0]
    cols = land_sea.shape[1]
    chans = fields.shape[2]
    north = shifted(fields[-1:], "lat", 1)
    edge_column = jnp.concatenate([north[:, -1:], fields[:, -1:]], axis=0)
    west = from_behind(edge_column, "lon", 1)
    phases = fields.reshape(rows, 2, cols, 2, chans)
    rows_even = phases[:, 0]
    rows_odd = phases[:, 1]
    rows_prev = jnp.concatenate([north.reshape(1, cols, 2, chans), rows_odd[:-1]], axis=0)
    row_sets = (rows_prev, rows_even, rows_odd)
    west_sets = (west[0 : 2 * rows : 2], west[1 : 2 * rows + 1 : 2], west[2 : 2 * rows + 1 : 2])
    down = jnp.zeros((rows, cols, chans), jnp.float32) + b_depth
    for a in range(3):
        chosen = row_sets[a]
        col_prev = jnp.concatenate([west_sets[a], chosen[:, :-1, 1]], axis=1)
        down = (
            down
            + col_prev * w_depth[a, 0]
            + chosen[:, :, 0] * w_depth[a, 1]
            + chosen[:, :, 1] * w_depth[a, 2]
        )
    mask = land_sea.astype(jnp.float32)[:, :, None]
    down_bf = (down * mask).astype(jnp.bfloat16)
    framed = padded(down_bf, (("lat", 0), ("lon", 1)), 4)
    framed = clear_poles(framed, 4, rows)
    hidden = jax.nn.gelu(dilated(framed, w_one, b_one, 4, rows, cols), approximate=False).astype(
        jnp.bfloat16
    )
    outer = padded(hidden, (("lat", 0), ("lon", 1)), 8)
    outer = clear_poles(outer, 8, rows)
    return jax.nn.gelu(dilated(outer, w_two, b_two, 8, rows, cols), approximate=False) * mask


def solution(mesh):
    return jax.shard_map(
        on_device,
        mesh=mesh,
        in_specs=(P("lat", "lon", None), P("lat", "lon"), P(), P(), P(), P(), P(), P()),
        out_specs=P("lat", "lon", None),
        check_vma=False,
    )
```

profile of v0, /device:TPU:31, one launch (start us, length us, event | category | flops | bytes accessed | tf_op | source)
XLA Modules:
  0.0 96.5 jit_solution(59120221987014102)
XLA Ops:
  0.0 0.8 slice.235
  0.8 4.0 %collective-permute-start = (f32[1,32,256]{2,1,0:T(8,128)S(1)}, f32[1,32,256]{2,1,0:T(8,128)S(1)}, u32[]{:S(2)}, u32[]{:S(2)}) collective-permute-start(f32[1,32,256]{2,1,0:T(8,128)S(1)} %slice.235), channel_id=1, source_target_pairs={{0,32},{32,64},{64,96},{96,128},{128,160},{160,192},{192,224},{224... | collective-permute-start | bytes 98312 | tf_op jit(solution)/shard_map/ppermute | solution.py:10
  4.8 2.5 %reshape.28 = f32[32,2,16,2,256]{4,3,2,1,0:T(2,128)S(1)} reshape(f32[64,32,256]{2,1,0:T(8,128)} %param.8) | data formatting | bytes 4194304 | tf_op jit(solution)/shard_map/reshape | solution.py:62
  7.3 0.7 fusion.78
  8.0 0.0 copy-start.7
  8.0 0.2 copy_bitcast_fusion
  8.2 0.0 copy-start.6
  8.2 0.9 slice_bitcast_fusion.2
  9.1 0.8 slice_bitcast_fusion.5
  10.0 0.6 fusion.83
  10.5 1.1 %slice.237 = f32[64,1,256]{2,1,0:T(1,128)S(1)} slice(f32[64,32,256]{2,1,0:T(8,128)} %param.8), slice={[0:64], [31:32], [0:256]} | slice | bytes 131072 | tf_op jit(solution)/shard_map/slice | solution.py:60
  11.6 1.3 %slice.314 = f32[31,1,16,2,256]{4,3,2,1,0:T(2,128)} slice(f32[32,2,16,2,256]{4,3,2,1,0:T(2,128)S(1)} %reshape.28), slice={[0:31], [1:2], [0:16], [0:2], [0:256]} | slice | bytes 2031616 | tf_op jit(solution)/shard_map/slice | solution.py:65
  12.9 0.1 copy.16
  13.0 1.4 %copy.24 = f32[31,1,16,2,256]{4,2,0,3,1:T(8,128)S(1)} copy(f32[31,1,16,2,256]{4,3,2,1,0:T(2,128)} %slice.314) | data formatting | bytes 2031616
  14.5 0.1 pad_maximum_fusion.5
  14.6 5.1 %collective-permute-start.1 = (f32[65,1,256]{2,1,0:T(1,128)S(1)}, f32[65,1,256]{2,1,0:T(1,128)S(1)}, u32[]{:S(2)}, u32[]{:S(2)}) collective-permute-start(f32[65,1,256]{2,1,0:T(1,128)S(1)} %pad_maximum_fusion.5), channel_id=1, source_target_pairs={{0,1},{1,2},{2,3},{3,4},{4,5},{5,6},{6,7},{7,8},{8,9},{9,10},{10,1... | collective-permute-start | bytes 199688 | tf_op jit(solution)/shard_map/ppermute | solution.py:15
  19.7 1.3 %collective-permute-done.1 = f32[65,1,256]{2,1,0:T(1,128)S(1)} collective-permute-done((f32[65,1,256]{2,1,0:T(1,128)S(1)}, f32[65,1,256]{2,1,0:T(1,128)S(1)}, u32[]{:S(2)}, u32[]{:S(2)}) %collective-permute-start.1) | collective-permute-done | bytes 66592 | tf_op jit(solution)/shard_map/ppermute | solution.py:15
  21.1 0.0 copy-start.5
  21.1 1.4 %fusion.56 = bf16[32,16,256]{2,1,0:T(8,128)(2,1)S(1)} fusion(f32[32,16,2,256]{3,1,0,2:T(8,128)S(1)} %get-tuple-element.45, f32[32,15,256]{2,1,0:T(8,128)S(1)} %copy-done.3, f32[32,1,256]{2,1,0:T(1,128)S(1)} %get-tuple-element.34, f32[32,16,2,256]{3,1,0,2:T(8,128)S(1)} %copy-done.1, f32[32,15,256]{2,1,0:T(8,128)S(1)} %copy-done.4, ...), kind=kLoop, calls=%fused_computation.114 | loop fusion | flops 3276800 | bytes 4993024 | tf_op jit(solution)/shard_map/convert_element_type | solution.py:79
  22.5 1.9 %collective-permute-start.2 = (bf16[4,16,256]{2,1,0:T(8,128)(2,1)S(1)}, bf16[4,16,256]{2,1,0:T(8,128)(2,1)S(1)}, u32[]{:S(2)}, u32[]{:S(2)}) collective-permute-start(bf16[4,16,256]{2,1,0:T(8,128)(2,1)S(1)} %get-tuple-element.31), channel_id=1, source_target_pairs={{0,32},{32,64},{64,96},{96,128},{128,160},{160,192},{192,224},{224... | collective-permute-start | bytes 98312 | tf_op jit(solution)/shard_map/ppermute | solution.py:25
  24.4 10.6 %collective-permute-start.3 = (bf16[4,16,256]{2,1,0:T(8,128)(2,1)S(1)}, bf16[4,16,256]{2,1,0:T(8,128)(2,1)S(1)}, u32[]{:S(2)}, u32[]{:S(2)}) collective-permute-start(bf16[4,16,256]{2,1,0:T(8,128)(2,1)S(1)} %get-tuple-element.32), channel_id=1, source_target_pairs={{32,0},{64,32},{96,64},{128,96},{160,128},{192,160},{224,192},{256... | collective-permute-start | bytes 98312 | tf_op jit(solution)/shard_map/ppermute | solution.py:27
  35.0 0.1 slice_bitcast_fusion.23
  35.1 0.9 collective-permute-done.3
  36.0 0.1 pad_maximum_fusion.4
  36.1 9.2 %collective-permute-start.4 = (bf16[40,4,256]{2,1,0:T(4,128)(2,1)S(1)}, bf16[40,4,256]{2,1,0:T(4,128)(2,1)S(1)}, u32[]{:S(2)}, u32[]{:S(2)}) collective-permute-start(bf16[40,4,256]{2,1,0:T(4,128)(2,1)S(1)} %get-tuple-element.29), channel_id=1, source_target_pairs={{0,1},{1,2},{2,3},{3,4},{4,5},{5,6},{6,7},{7,8},{8,9},{9,10},{10,1... | collective-permute-start | bytes 245768 | tf_op jit(solution)/shard_map/ppermute | solution.py:25
  45.3 1.9 %collective-permute-start.5 = (bf16[40,4,256]{2,1,0:T(4,128)(2,1)S(1)}, bf16[40,4,256]{2,1,0:T(4,128)(2,1)S(1)}, u32[]{:S(2)}, u32[]{:S(2)}) collective-permute-start(bf16[40,4,256]{2,1,0:T(4,128)(2,1)S(1)} %get-tuple-element.30), channel_id=1, source_target_pairs={{1,0},{2,1},{3,2},{4,3},{5,4},{6,5},{7,6},{8,7},{9,8},{10,9},{11,1... | collective-permute-start | bytes 245768 | tf_op jit(solution)/shard_map/ppermute | solution.py:27
  47.3 7.7 %collective-permute-done.5 = bf16[40,4,256]{2,1,0:T(4,128)(2,1)S(1)} collective-permute-done((bf16[40,4,256]{2,1,0:T(4,128)(2,1)S(1)}, bf16[40,4,256]{2,1,0:T(4,128)(2,1)S(1)}, u32[]{:S(2)}, u32[]{:S(2)}) %collective-permute-start.5) | collective-permute-done | bytes 81952 | tf_op jit(solution)/shard_map/ppermute | solution.py:27
  55.0 0.6 fusion.62
  55.6 0.6 fusion.67
  56.2 0.0 copy-start.9
  56.2 0.6 fusion.57
  56.9 0.0 copy-done.9
  56.9 2.7 %fusion.2 = bf16[32,16,300]{2,1,0:T(8,128)(2,1)S(1)} fusion(f32[32,24,900]{2,1,0:T(8,128)S(1)} %fusion.67, f32[32,24,900]{2,1,0:T(8,128)S(1)} %fusion.62, f32[32,24,900]{2,1,0:T(8,128)S(1)} %fusion.57, f32[300]{0:T(512)S(1)} %copy-done.9), kind=kLoop, calls=%fused_computation.12 | loop fusion | flops 11366400 | bytes 5838000 | tf_op jit(solution)/shard_map/convert_element_type | solution.py:82
  59.6 2.1 %collective-permute-start.6 = (bf16[8,16,300]{2,1,0:T(8,128)(2,1)S(1)}, bf16[8,16,300]{2,1,0:T(8,128)(2,1)S(1)}, u32[]{:S(2)}, u32[]{:S(2)}) collective-permute-start(bf16[8,16,300]{2,1,0:T(8,128)(2,1)S(1)} %get-tuple-element.27), channel_id=1, source_target_pairs={{0,32},{32,64},{64,96},{96,128},{128,160},{160,192},{192,224},{224... | collective-permute-start | bytes 230408 | tf_op jit(solution)/shard_map/ppermute | solution.py:25
  61.7 10.2 %collective-permute-start.7 = (bf16[8,16,300]{2,1,0:T(8,128)(2,1)S(1)}, bf16[8,16,300]{2,1,0:T(8,128)(2,1)S(1)}, u32[]{:S(2)}, u32[]{:S(2)}) collective-permute-start(bf16[8,16,300]{2,1,0:T(8,128)(2,1)S(1)} %get-tuple-element.28), channel_id=1, source_target_pairs={{32,0},{64,32},{96,64},{128,96},{160,128},{192,160},{224,192},{256... | collective-permute-start | bytes 230408 | tf_op jit(solution)/shard_map/ppermute | solution.py:27
  71.9 0.0 collective-permute-done.6
  72.0 1.6 %collective-permute-done.7 = bf16[8,16,300]{2,1,0:T(8,128)(2,1)S(1)} collective-permute-done((bf16[8,16,300]{2,1,0:T(8,128)(2,1)S(1)}, bf16[8,16,300]{2,1,0:T(8,128)(2,1)S(1)}, u32[]{:S(2)}, u32[]{:S(2)}) %collective-permute-start.7) | collective-permute-done | bytes 76832 | tf_op jit(solution)/shard_map/ppermute | solution.py:27
  73.5 0.1 pad_maximum_fusion
  73.7 0.1 fusion.79
  73.7 3.6 %collective-permute-start.8 = (bf16[48,8,300]{2,1,0:T(8,128)(2,1)S(1)}, bf16[48,8,300]{2,1,0:T(8,128)(2,1)S(1)}, u32[]{:S(2)}, u32[]{:S(2)}) collective-permute-start(bf16[48,8,300]{2,1,0:T(8,128)(2,1)S(1)} %get-tuple-element.25), channel_id=1, source_target_pairs={{0,1},{1,2},{2,3},{3,4},{4,5},{5,6},{6,7},{7,8},{8,9},{9,10},{10,1... | collective-permute-start | bytes 691208 | tf_op jit(solution)/shard_map/ppermute | solution.py:25
  77.4 2.1 %collective-permute-start.9 = (bf16[48,8,300]{2,1,0:T(8,128)(2,1)S(1)}, bf16[48,8,300]{2,1,0:T(8,128)(2,1)S(1)}, u32[]{:S(2)}, u32[]{:S(2)}) collective-permute-start(bf16[48,8,300]{2,1,0:T(8,128)(2,1)S(1)} %get-tuple-element.26), channel_id=1, source_target_pairs={{1,0},{2,1},{3,2},{4,3},{5,4},{6,5},{7,6},{8,7},{9,8},{10,9},{11,1... | collective-permute-start | bytes 691208 | tf_op jit(solution)/shard_map/ppermute | solution.py:27
  79.5 0.2 slice_bitcast_fusion.14
  79.7 3.6 %collective-permute-done.8 = bf16[48,8,300]{2,1,0:T(8,128)(2,1)S(1)} collective-permute-done((bf16[48,8,300]{2,1,0:T(8,128)(2,1)S(1)}, bf16[48,8,300]{2,1,0:T(8,128)(2,1)S(1)}, u32[]{:S(2)}, u32[]{:S(2)}) %collective-permute-start.8) | collective-permute-done | bytes 230432 | tf_op jit(solution)/shard_map/ppermute | solution.py:25
  83.3 6.0 %collective-permute-done.9 = bf16[48,8,300]{2,1,0:T(8,128)(2,1)S(1)} collective-permute-done((bf16[48,8,300]{2,1,0:T(8,128)(2,1)S(1)}, bf16[48,8,300]{2,1,0:T(8,128)(2,1)S(1)}, u32[]{:S(2)}, u32[]{:S(2)}) %collective-permute-start.9) | collective-permute-done | bytes 230432 | tf_op jit(solution)/shard_map/ppermute | solution.py:27
  89.3 1.3 %fusion.25 = f32[32,32,900]{2,1,0:T(8,128)S(1)} fusion(bf16[300,300]{1,0:T(8,128)(2,1)S(1)} %get-tuple-element.7, bf16[300,300]{1,0:T(8,128)(2,1)S(1)} %get-tuple-element.8, bf16[300,300]{1,0:T(8,128)(2,1)S(1)} %get-tuple-element.9, bf16[48,8,300]{2,1,0:T(8,128)(2,1)S(1)} %collective-permute-done.9, bf16[8,16,300]{2,1,0:T(8,128)(2,1)S(1)} %collective-permute-done.7, ...), kind=kOutput, calls=%fused_computation.71 | convolution fusion | flops 559648768 | bytes 5148048 | tf_op jit(solution)/shard_map/ijc,cd->ijd/dot_general | solution.py:49
  90.7 1.3 %fusion.30 = f32[32,32,900]{2,1,0:T(8,128)S(1)} fusion(bf16[300,300]{1,0:T(8,128)(2,1)S(1)} %get-tuple-element.12, bf16[300,300]{1,0:T(8,128)(2,1)S(1)} %get-tuple-element.13, bf16[300,300]{1,0:T(8,128)(2,1)S(1)} %get-tuple-element.6, bf16[48,8,300]{2,1,0:T(8,128)(2,1)S(1)} %collective-permute-done.9, bf16[8,16,300]{2,1,0:T(8,128)(2,1)S(1)} %collective-permute-done.7, ...), kind=kOutput, calls=%fused_computation.77 | convolution fusion | flops 559648768 | bytes 5148048 | tf_op jit(solution)/shard_map/ijc,cd->ijd/dot_general | solution.py:49
  92.0 1.3 %fusion.20 = f32[32,32,900]{2,1,0:T(8,128)S(1)} fusion(bf16[300,300]{1,0:T(8,128)(2,1)S(1)} %get-tuple-element.10, bf16[300,300]{1,0:T(8,128)(2,1)S(1)} %get-tuple-element.11, bf16[300,300]{1,0:T(8,128)(2,1)S(1)} %get-tuple-element.5, bf16[48,8,300]{2,1,0:T(8,128)(2,1)S(1)} %collective-permute-done.9, bf16[8,16,300]{2,1,0:T(8,128)(2,1)S(1)} %collective-permute-done.7, ...), kind=kOutput, calls=%fused_computation.65 | convolution fusion | flops 559648768 | bytes 5148048 | tf_op jit(solution)/shard_map/ijc,cd->ijd/dot_general | solution.py:49
  93.4 3.1 %fusion.5 = f32[32,16,300]{2,1,0:T(8,128)} fusion(f32[32,32,900]{2,1,0:T(8,128)S(1)} %fusion.30, f32[32,32,900]{2,1,0:T(8,128)S(1)} %fusion.25, f32[32,32,900]{2,1,0:T(8,128)S(1)} %fusion.20, f32[32,16]{1,0:T(8,128)S(1)} %copy.16, f32[300]{0:T(512)S(1)} %copy-done.8), kind=kLoop, calls=%fused_computation.15 | loop fusion | flops 11366400 | bytes 6147248 | tf_op jit(solution)/shard_map/mul | solution.py:87
  (28 shorter events, 0.2 us)
Async XLA Ops:
  0.8 13.7 %collective-permute-start = (f32[1,32,256]{2,1,0:T(8,128)S(1)}, f32[1,32,256]{2,1,0:T(8,128)S(1)}, u32[]{:S(2)}, u32[]{:S(2)}) collective-permute-start(f32[1,32,256]{2,1,0:T(8,128)S(1)} %slice.235), channel_id=1, source_target_pairs={{0,32},{32,64},{64,96},{96,128},{128,160},{160,192},{192,224},{224... | collective-permute-start | bytes 98312 | tf_op jit(solution)/shard_map/ppermute | solution.py:10
  8.0 2.0 %copy-start.7 = (f32[3,3,256]{2,1,0:T(4,128)S(1)}, f32[3,3,256]{2,1,0:T(4,128)}, u32[]{:S(2)}) copy-start(f32[3,3,256]{2,1,0:T(4,128)} %param.10) | copy-start | bytes 27652
  8.2 4.7 %copy-start = (f32[32,16,2,256]{3,1,0,2:T(8,128)}, f32[32,16,2,256]{3,1,0,2:T(8,128)S(1)}, u32[]{:S(2)}) copy-start(f32[32,16,2,256]{3,1,0,2:T(8,128)S(1)} %get-tuple-element.46) | copy-start | bytes 3145732
  8.2 4.7 %copy-start.6 = (s32[32,16]{0,1:T(8,128)S(1)}, s32[32,16]{0,1:T(8,128)}, u32[]{:S(2)}) copy-start(s32[32,16]{0,1:T(8,128)} %param.9) | copy-start | bytes 6148
  12.9 8.2 %copy-start.3 = (f32[32,15,256]{2,1,0:T(8,128)S(1)}, f32[32,15,256]{2,1,0:T(8,128)}, u32[]{:S(2)}) copy-start(f32[32,15,256]{2,1,0:T(8,128)} %slice_bitcast_fusion.2) | copy-start | bytes 1474564
  12.9 8.2 %copy-start.4 = (f32[32,15,256]{2,1,0:T(8,128)S(1)}, f32[32,15,256]{2,1,0:T(8,128)}, u32[]{:S(2)}) copy-start(f32[32,15,256]{2,1,0:T(8,128)} %slice_bitcast_fusion.5) | copy-start | bytes 1474564
  14.5 6.6 %copy-start.1 = (f32[32,16,2,256]{3,1,0,2:T(8,128)S(1)}, f32[32,16,2,256]{3,1,0,2:T(8,128)}, u32[]{:S(2)}) copy-start(f32[32,16,2,256]{3,1,0,2:T(8,128)} %copy-done) | copy-start | bytes 3145732
  14.6 6.5 %collective-permute-start.1 = (f32[65,1,256]{2,1,0:T(1,128)S(1)}, f32[65,1,256]{2,1,0:T(1,128)S(1)}, u32[]{:S(2)}, u32[]{:S(2)}) collective-permute-start(f32[65,1,256]{2,1,0:T(1,128)S(1)} %pad_maximum_fusion.5), channel_id=1, source_target_pairs={{0,1},{1,2},{2,3},{3,4},{4,5},{5,6},{6,7},{7,8},{8,9},{9,10},{10,1... | collective-permute-start | bytes 199688 | tf_op jit(solution)/shard_map/ppermute | solution.py:15
  21.1 13.9 %copy-start.5 = (bf16[3,3,256,300]{2,3,1,0:T(8,128)(2,1)S(1)}, bf16[3,3,256,300]{2,3,1,0:T(8,128)(2,1)}, u32[]{:S(2)}) copy-start(bf16[3,3,256,300]{2,3,1,0:T(8,128)(2,1)} %param.12) | copy-start | bytes 4147204
  22.5 12.6 %collective-permute-start.2 = (bf16[4,16,256]{2,1,0:T(8,128)(2,1)S(1)}, bf16[4,16,256]{2,1,0:T(8,128)(2,1)S(1)}, u32[]{:S(2)}, u32[]{:S(2)}) collective-permute-start(bf16[4,16,256]{2,1,0:T(8,128)(2,1)S(1)} %get-tuple-element.31), channel_id=1, source_target_pairs={{0,32},{32,64},{64,96},{96,128},{128,160},{160,192},{192,224},{224... | collective-permute-start | bytes 98312 | tf_op jit(solution)/shard_map/ppermute | solution.py:25
  24.4 11.6 %collective-permute-start.3 = (bf16[4,16,256]{2,1,0:T(8,128)(2,1)S(1)}, bf16[4,16,256]{2,1,0:T(8,128)(2,1)S(1)}, u32[]{:S(2)}, u32[]{:S(2)}) collective-permute-start(bf16[4,16,256]{2,1,0:T(8,128)(2,1)S(1)} %get-tuple-element.32), channel_id=1, source_target_pairs={{32,0},{64,32},{96,64},{128,96},{160,128},{192,160},{224,192},{256... | collective-permute-start | bytes 98312 | tf_op jit(solution)/shard_map/ppermute | solution.py:27
  36.1 11.2 %collective-permute-start.4 = (bf16[40,4,256]{2,1,0:T(4,128)(2,1)S(1)}, bf16[40,4,256]{2,1,0:T(4,128)(2,1)S(1)}, u32[]{:S(2)}, u32[]{:S(2)}) collective-permute-start(bf16[40,4,256]{2,1,0:T(4,128)(2,1)S(1)} %get-tuple-element.29), channel_id=1, source_target_pairs={{0,1},{1,2},{2,3},{3,4},{4,5},{5,6},{6,7},{7,8},{8,9},{9,10},{10,1... | collective-permute-start | bytes 245768 | tf_op jit(solution)/shard_map/ppermute | solution.py:25
  45.3 9.7 %collective-permute-start.5 = (bf16[40,4,256]{2,1,0:T(4,128)(2,1)S(1)}, bf16[40,4,256]{2,1,0:T(4,128)(2,1)S(1)}, u32[]{:S(2)}, u32[]{:S(2)}) collective-permute-start(bf16[40,4,256]{2,1,0:T(4,128)(2,1)S(1)} %get-tuple-element.30), channel_id=1, source_target_pairs={{1,0},{2,1},{3,2},{4,3},{5,4},{6,5},{7,6},{8,7},{9,8},{10,9},{11,1... | collective-permute-start | bytes 245768 | tf_op jit(solution)/shard_map/ppermute | solution.py:27
  56.2 0.7 copy-start.9
  59.6 19.9 %copy-start.2 = (bf16[3,3,300,300]{3,2,1,0:T(8,128)(2,1)S(1)}, bf16[3,3,300,300]{3,2,1,0:T(8,128)(2,1)}, u32[]{:S(2)}) copy-start(bf16[3,3,300,300]{3,2,1,0:T(8,128)(2,1)} %param.14) | copy-start | bytes 4860004
  59.6 12.4 %collective-permute-start.6 = (bf16[8,16,300]{2,1,0:T(8,128)(2,1)S(1)}, bf16[8,16,300]{2,1,0:T(8,128)(2,1)S(1)}, u32[]{:S(2)}, u32[]{:S(2)}) collective-permute-start(bf16[8,16,300]{2,1,0:T(8,128)(2,1)S(1)} %get-tuple-element.27), channel_id=1, source_target_pairs={{0,32},{32,64},{64,96},{96,128},{128,160},{160,192},{192,224},{224... | collective-permute-start | bytes 230408 | tf_op jit(solution)/shard_map/ppermute | solution.py:25
  61.7 11.9 %collective-permute-start.7 = (bf16[8,16,300]{2,1,0:T(8,128)(2,1)S(1)}, bf16[8,16,300]{2,1,0:T(8,128)(2,1)S(1)}, u32[]{:S(2)}, u32[]{:S(2)}) collective-permute-start(bf16[8,16,300]{2,1,0:T(8,128)(2,1)S(1)} %get-tuple-element.28), channel_id=1, source_target_pairs={{32,0},{64,32},{96,64},{128,96},{160,128},{192,160},{224,192},{256... | collective-permute-start | bytes 230408 | tf_op jit(solution)/shard_map/ppermute | solution.py:27
  73.7 9.6 %collective-permute-start.8 = (bf16[48,8,300]{2,1,0:T(8,128)(2,1)S(1)}, bf16[48,8,300]{2,1,0:T(8,128)(2,1)S(1)}, u32[]{:S(2)}, u32[]{:S(2)}) collective-permute-start(bf16[48,8,300]{2,1,0:T(8,128)(2,1)S(1)} %get-tuple-element.25), channel_id=1, source_target_pairs={{0,1},{1,2},{2,3},{3,4},{4,5},{5,6},{6,7},{7,8},{8,9},{9,10},{10,1... | collective-permute-start | bytes 691208 | tf_op jit(solution)/shard_map/ppermute | solution.py:25
  77.4 11.9 %collective-permute-start.9 = (bf16[48,8,300]{2,1,0:T(8,128)(2,1)S(1)}, bf16[48,8,300]{2,1,0:T(8,128)(2,1)S(1)}, u32[]{:S(2)}, u32[]{:S(2)}) collective-permute-start(bf16[48,8,300]{2,1,0:T(8,128)(2,1)S(1)} %get-tuple-element.26), channel_id=1, source_target_pairs={{1,0},{2,1},{3,2},{4,3},{5,4},{6,5},{7,6},{8,7},{9,8},{10,9},{11,1... | collective-permute-start | bytes 691208 | tf_op jit(solution)/shard_map/ppermute | solution.py:27
  92.0 1.4 %copy-start.8 = (f32[300]{0:T(512)S(1)}, f32[300]{0:T(512)}, u32[]{:S(2)}) copy-start(f32[300]{0:T(512)} %param.15) | copy-start | bytes 3604
where the time goes:
time: 97.1 us; the launch traced here: 96.5 us
  starting transfers between devices  50.7 us (52%)
  waiting for transfers between devices  21.1 us (22%)
  local copies, waits for them, and re-layouts  10.9 us (11%)
  other arithmetic  7.48 us (8%)
  matrix products  5.89 us (6%)
    ppermute x4, starting transfers between devices, padded(): lax.ppermute(head, axis, [((i + 1) % count, i) for i in range(count)])  24.8 us
    ppermute x4, starting transfers between devices, padded(): lax.ppermute(tail, axis, [(i, (i + 1) % count) for i in range(count)])  16.8 us
    ppermute x4, waiting for transfers between devices, padded(): lax.ppermute(head, axis, [((i + 1) % count, i) for i in range(count)])  16.2 us
    dot_general x6, matrix products, dilated(): jnp.einsum('ijc,cd->ijd', band, taps, preferred_element_type=jnp.float32)  5.89 us
    ppermute x1, starting transfers between devices, from_behind(): lax.ppermute(array, axis, [(i, (i + by) % devices) for i in range(devices)])  5.12 us
    ppermute x1, starting transfers between devices, shifted(): return lax.ppermute(block, axis, route)  3.99 us
    ppermute x4, waiting for transfers between devices, padded(): lax.ppermute(tail, axis, [(i, (i + 1) % count) for i in range(count)])  3.64 us
    mul x1, other arithmetic, on_device(): jax.nn.gelu(dilated(outer, w_two, b_two, 8, rows, cols), approximate=False)  3.13 us
  transfers between devices with their start and end apart: 10, of which 6 were waited for; matrix products, arithmetic and copies ran while one was open for 10% of the time, Pallas kernels for 0%

commit v1 on v0

v1 whole, which is shorter than its diff:
```python
import jax
import jax.numpy as jnp
from jax import lax
from jax.experimental import pallas as pl
from jax.experimental.pallas import tpu as pltpu
from jax.sharding import PartitionSpec as P

ROWS = 32
COLS = 16
HALO = 12
EXT_R = ROWS + 2 * HALO
EXT_C = COLS + 2 * HALO
HID_R = ROWS + 16
HID_C = COLS + 16
PACK = EXT_R * HALO
MASKED = 2.0**100
LIMIT = 2.0**90
F32 = jnp.float32
BF16 = jnp.bfloat16


def mask_column(mask_row, eye):
    return jnp.sum(jnp.where(eye, mask_row, 0), axis=1, keepdims=True)


def down_kernel(f_ref, ls_ref, wd_ref, bd_ref, own_ref, edge_ref, south_ref, north_ref, edge):
    last = lax.axis_index("lat") == lax.axis_size("lat") - 1
    chans = f_ref.shape[2]
    sub = lax.broadcasted_iota(jnp.int32, (COLS, chans), 0)
    first = sub == 0
    eye = lax.broadcasted_iota(jnp.int32, (COLS, COLS), 0) == lax.broadcasted_iota(
        jnp.int32, (COLS, COLS), 1
    )
    weight = [[wd_ref[a, b : b + 1, :] for b in range(3)] for a in range(3)]
    bias = bd_ref[...]

    def terms(r, a):
        even = f_ref[r, pl.ds(0, COLS, stride=2), :]
        odd = f_ref[r, pl.ds(1, COLS, stride=2), :]
        return even * weight[a][1] + odd * weight[a][2], odd * weight[a][0]

    def put(i, here, after, masked):
        moved = pltpu.roll(after, 1, 0)
        edge[pl.ds(i, 1), :] = moved[0:1, :]
        value = here + jnp.where(first, 0.0, moved)
        if masked is not None:
            keep = mask_column(ls_ref[pl.ds(i, 1), :], eye) != 0
            value = jnp.where(keep, value, masked)
        own_ref[i] = value.astype(BF16)

    edge[...] = jnp.zeros_like(edge)
    h1, p1 = terms(0, 1)
    h2, p2 = terms(1, 2)
    put(0, h1 + h2 + bias, p1 + p2, jnp.full((COLS, chans), MASKED, F32))
    holed = jnp.where(first, MASKED, 0.0)

    def row(i, _):
        h0, p0 = terms(2 * i - 1, 0)
        h1, p1 = terms(2 * i, 1)
        h2, p2 = terms(2 * i + 1, 2)
        put(i, h0 + h1 + h2 + bias, p0 + p1 + p2, holed)
        return 0

    lax.fori_loop(1, ROWS, row, 0)
    h0, p0 = terms(2 * ROWS - 1, 0)
    scale = jnp.where(last, 0.0, 1.0)
    put(ROWS, h0 * scale, p0 * scale, None)

    edge_ref[...] = edge[...].astype(BF16)
    south_ref[0 : HALO + 1] = own_ref[ROWS - HALO : ROWS + 1]
    south_ref[HALO + 1] = edge[ROWS - HALO : ROWS - HALO + 16, :].astype(BF16)
    north_ref[0:HALO] = own_ref[0:HALO]
    north_ref[HALO] = edge[0:16, :].astype(BF16)


def band_kernel(own_ref, edge_ref, n_ref, s_ref, band_ref, col_ref, east_ref, west_ref, te, tw, col):
    col[HALO : HALO + ROWS + 16] = edge_ref[...].astype(F32)
    n_edge = n_ref[HALO + 1].astype(F32)
    s_edge = s_ref[HALO].astype(F32)
    col[0:HALO] = n_edge[0:HALO]
    col[HALO : HALO + 1] += n_edge[HALO : HALO + 1]
    col[HALO + ROWS : HALO + ROWS + 1] += s_edge[0:1]
    col[HALO + ROWS + 1 : EXT_R] = s_edge[1:HALO]

    def put(r, value):
        band_ref[r] = value.astype(BF16)
        te[r * HALO : (r + 1) * HALO] = value[COLS - HALO :]
        tw[r * HALO : (r + 1) * HALO] = value[:HALO]

    for r in range(EXT_R):
        i = r - HALO
        if i < 0:
            put(r, n_ref[r].astype(F32))
        elif i == 0:
            put(r, own_ref[0].astype(F32) + n_ref[HALO].astype(F32))
        elif i < ROWS:
            put(r, own_ref[i].astype(F32))
        elif i == ROWS:
            put(r, own_ref[ROWS].astype(F32) + s_ref[0].astype(F32))
        else:
            put(r, s_ref[i - ROWS].astype(F32))
    te[PACK : PACK + 64] = col[...]
    col_ref[...] = col[...].astype(BF16)
    east_ref[...] = te[...].astype(BF16)
    west_ref[...] = tw[...].astype(BF16)


def gelu(x):
    return 0.5 * x * (1.0 + lax.erf(x * (0.5**0.5)))


def conv_kernel(
    band_ref, col_ref, w_ref, e_ref, ls_ref, w1_ref, b1_ref, w2_ref, b2_ref, out_ref,
    tw, te, col, ext, db, h0, h8,
):
    lat = lax.axis_index("lat")
    last = lax.axis_size("lat") - 1
    out_ch = b1_ref.shape[1]
    tw[...] = w_ref[...].astype(F32)
    te[...] = e_ref[...].astype(F32)
    col[...] = col_ref[...].astype(F32)

    for r in range(EXT_R):
        ext[r, 0:HALO] = tw[r * HALO : (r + 1) * HALO]
        ext[r, HALO : HALO + COLS] = band_ref[r].astype(F32)
        ext[r, HALO + COLS : EXT_C] = te[r * HALO : (r + 1) * HALO]
        ext[r, HALO : HALO + 1] += tw[PACK + r : PACK + r + 1]
        ext[r, HALO + COLS : HALO + COLS + 1] += col[r : r + 1]
    for r in range(EXT_R):
        for b in range(3):
            piece = ext[r, 4 * b : 4 * b + HID_C]
            db[b, r] = jnp.where(piece > LIMIT, 0.0, piece).astype(BF16)

    step = 8

    def first(k, _):
        r0 = pl.multiple_of(k * step, step)
        total = jnp.zeros((step * HID_C, out_ch), F32) + b1_ref[...]
        for a in range(3):
            for b in range(3):
                piece = db[b, pl.ds(r0 + 4 * a, step)].reshape(step * HID_C, -1)
                total = total + jnp.dot(piece, w1_ref[a, b], preferred_element_type=F32)
        inside = jnp.logical_and(
            jnp.logical_or(k > 0, lat > 0),
            jnp.logical_or(k < HID_R // step - 1, lat < last),
        )
        value = gelu(total) * jnp.where(inside, 1.0, 0.0)
        value = value.reshape(step, HID_C, out_ch)
        h0[pl.ds(r0, step)] = value.astype(BF16)
        h8[pl.ds(r0, step)] = value[:, 8:24].astype(BF16)
        return 0

    lax.fori_loop(0, HID_R // step, first, 0)

    eye = lax.broadcasted_iota(jnp.int32, (COLS, COLS), 0) == lax.broadcasted_iota(
        jnp.int32, (COLS, COLS), 1
    )
    half = 16
    for k in range(ROWS // half):
        total = jnp.zeros((half * COLS, out_ch), F32) + b2_ref[...]
        for a in range(3):
            for b in range(3):
                rows = pl.ds(k * half + 8 * a, half)
                if b == 0:
                    piece = h0[rows, 0:COLS]
                elif b == 1:
                    piece = h8[rows]
                else:
                    piece = h0[rows, COLS : 2 * COLS]
                piece = piece.reshape(half * COLS, out_ch)
                total = total + jnp.dot(piece, w2_ref[a, b], preferred_element_type=F32)
        value = gelu(total).reshape(half, COLS, out_ch)
        for i in range(half):
            keep = mask_column(ls_ref[k * half + i : k * half + i + 1, :], eye)
            out_ref[k * half + i] = value[i] * keep.astype(F32)


def line(axis, by):
    count = lax.axis_size(axis)
    return [(i, i + by) for i in range(count) if 0 <= i + by < count]


def ring(axis, by):
    count = lax.axis_size(axis)
    return [(i, (i + by) % count) for i in range(count)]


def on_device(fields, land_sea, w_depth, b_depth, w_one, b_one, w_two, b_two):
    chans = fields.shape[2]
    out_ch = w_one.shape[3]
    vmem = pl.BlockSpec(memory_space=pltpu.VMEM)

    def shape(*dims, dtype=BF16):
        return jax.ShapeDtypeStruct(dims, dtype)

    lanes = 128

    def part(*dims):
        zeros = (0,) * len(dims)
        return pl.BlockSpec((*dims, lanes), lambda c: (*zeros, c))

    own, edge, south, north = pl.pallas_call(
        down_kernel,
        grid=(chans // lanes,),
        out_shape=(
            shape(ROWS + 1, COLS, chans),
            shape(ROWS + 16, chans),
            shape(HALO + 2, COLS, chans),
            shape(HALO + 1, COLS, chans),
        ),
        in_specs=[
            part(2 * ROWS, 2 * COLS),
            pl.BlockSpec((ROWS, COLS), lambda c: (0, 0)),
            part(3, 3),
            part(1),
        ],
        out_specs=[
            part(ROWS + 1, COLS),
            part(ROWS + 16),
            part(HALO + 2, COLS),
            part(HALO + 1, COLS),
        ],
        scratch_shapes=[pltpu.VMEM((ROWS + 16, lanes), F32)],
        compiler_params=pltpu.CompilerParams(vmem_limit_bytes=16 << 20),
        name="down",
    )(fields, land_sea, w_depth, b_depth[None])

    from_north = lax.ppermute(south, "lat", line("lat", 1))
    from_south = lax.ppermute(north, "lat", line("lat", -1))

    band, col, east, west = pl.pallas_call(
        band_kernel,
        out_shape=(
            shape(EXT_R, COLS, chans),
            shape(64, chans),
            shape(PACK + 64, chans),
            shape(PACK, chans),
        ),
        in_specs=[vmem] * 4,
        out_specs=[vmem] * 4,
        scratch_shapes=[
            pltpu.VMEM((PACK + 64, chans), F32),
            pltpu.VMEM((PACK, chans), F32),
            pltpu.VMEM((64, chans), F32),
        ],
        compiler_params=pltpu.CompilerParams(vmem_limit_bytes=16 << 20),
        name="band",
    )(own, edge, from_north, from_south)

    from_west = lax.ppermute(east, "lon", ring("lon", 1))
    from_east = lax.ppermute(west, "lon", ring("lon", -1))

    return pl.pallas_call(
        conv_kernel,
        out_shape=shape(ROWS, COLS, out_ch, dtype=F32),
        in_specs=[vmem] * 9,
        out_specs=vmem,
        scratch_shapes=[
            pltpu.VMEM((PACK + 64, chans), F32),
            pltpu.VMEM((PACK, chans), F32),
            pltpu.VMEM((64, chans), F32),
            pltpu.VMEM((EXT_R, EXT_C, chans), F32),
            pltpu.VMEM((3, EXT_R, HID_C, chans), BF16),
            pltpu.VMEM((HID_R, HID_C, out_ch), BF16),
            pltpu.VMEM((HID_R, COLS, out_ch), BF16),
        ],
        compiler_params=pltpu.CompilerParams(vmem_limit_bytes=32 << 20),
        name="convolve",
    )(band, col, from_west, from_east, land_sea, w_one, b_one[None], w_two, b_two[None])


def solution(mesh):
    return jax.shard_map(
        on_device,
        mesh=mesh,
        in_specs=(P("lat", "lon", None), P("lat", "lon"), P(), P(), P(), P(), P(), P()),
        out_specs=P("lat", "lon", None),
        check_vma=False,
    )
```

time: 97.1 us -> 54.1 us (0.56)
  the two profiles are of different devices: /device:TPU:31 before, /device:TPU:57 now
where the time goes in v1:
time: 54.1 us; the launch traced here: 53.5 us
  starting transfers between devices  20.9 us (39%)
  Pallas kernels  15.8 us (29%)
  waiting for transfers between devices  8.63 us (16%)
  local copies, waits for them, and re-layouts  8.05 us (15%)
    ppermute x1, starting transfers between devices, on_device(): from_south = lax.ppermute(north, 'lat', line('lat', -1))  10.8 us
    pallas_call x1, Pallas kernels, on_device(): pl.pallas_call(conv_kernel, out_shape=shape(ROWS, COLS, out_ch, dtype=F32...  9.03 us
    unnamed x14, local copies, waits for them, and re-layouts  8.05 us
    ppermute x1, waiting for transfers between devices, on_device(): from_east = lax.ppermute(west, 'lon', ring('lon', -1))  6.93 us
    pallas_call x1, Pallas kernels, on_device(): pl.pallas_call(down_kernel, grid=(chans // lanes,), out_shape=(shape(ROWS...  5.87 us
    ppermute x1, starting transfers between devices, on_device(): from_west = lax.ppermute(east, 'lon', ring('lon', 1))  4.18 us
    ppermute x1, starting transfers between devices, on_device(): from_north = lax.ppermute(south, 'lat', line('lat', 1))  4 us
    ppermute x1, starting transfers between devices, on_device(): from_east = lax.ppermute(west, 'lon', ring('lon', -1))  1.92 us
  transfers between devices with their start and end apart: 4, of which 2 were waited for; matrix products, arithmetic and copies ran while one was open for 5% of the time, Pallas kernels for 0%

profile of v1, /device:TPU:57, one launch (start us, length us, event | category | flops | bytes accessed | tf_op | source)
XLA Modules:
  0.0 53.5 jit_solution(5350219142373313921)
XLA Ops:
  0.0 0.0 copy-start.4
  0.0 0.0 copy-start.5
  0.0 0.8 %copy.9.ls_ref = s32[32,16]{1,0:T(8,128)S(1)} copy(s32[32,16]{0,1:T(8,128)} %param.9) | data formatting | bytes 4096 | tf_op args[1]
  0.8 0.0 copy-start.1
  0.8 1.6 %copy-done.1 = f32[64,32,256]{2,1,0:T(8,128)S(1)} copy-done((f32[64,32,256]{2,1,0:T(8,128)S(1)}, f32[64,32,256]{2,1,0:T(8,128)}, u32[]{:S(2)}) %copy-start.1) | copy-done | bytes 2097176
  2.4 0.0 copy-start.2
  2.4 0.7 %copy-done.2 = f32[3,3,256]{2,1,0:T(4,128)S(1)} copy-done((f32[3,3,256]{2,1,0:T(4,128)S(1)}, f32[3,3,256]{2,1,0:T(4,128)}, u32[]{:S(2)}) %copy-start.2) | copy-done | bytes 9240
  3.1 0.0 copy-start.3
  3.1 0.7 %copy-done.3 = f32[256]{0:T(256)S(1)} copy-done((f32[256]{0:T(256)S(1)}, f32[256]{0:T(256)}, u32[]{:S(2)}) %copy-start.3) | copy-done | bytes 1048
  3.8 5.9 %down.1 = (bf16[33,16,256]{2,1,0:T(8,128)(2,1)S(1)}, bf16[48,256]{1,0:T(8,128)(2,1)S(1)}, bf16[14,16,256]{2,1,0:T(8,128)(2,1)S(1)}, bf16[13,16,256]{2,1,0:T(8,128)(2,1)S(1)}) custom-call(f32[64,32,256]{2,1,0:T(8,128)S(1)} %copy-done.1, s32[32,16]{1,0:T(8,128)S(1)} %copy.9.ls_ref, f32[3,3,256]{2,1,0:T(4,128)S(1)} %copy-done.2, f32[1,256]{1,0:T(1,128)S(1)} %bitcast.1), custom_call_target="tpu_custom_call" | custom-call | tf_op jit(solution)/shard_map/down/pallas_call | solution.py:202
  9.7 4.0 %collective-permute-start = (bf16[14,16,256]{2,1,0:T(8,128)(2,1)S(1)}, bf16[14,16,256]{2,1,0:T(8,128)(2,1)S(1)}, u32[]{:S(2)}, u32[]{:S(2)}) collective-permute-start(bf16[14,16,256]{2,1,0:T(8,128)(2,1)S(1)} %get-tuple-element.15), channel_id=1, source_target_pairs={{0,32},{32,64},{64,96},{96,128},{128,160},{160,192},{192,224},{224... | collective-permute-start | bytes 344072 | tf_op jit(solution)/shard_map/ppermute | solution.py:228
  13.7 10.8 %collective-permute-start.1 = (bf16[13,16,256]{2,1,0:T(8,128)(2,1)S(1)}, bf16[13,16,256]{2,1,0:T(8,128)(2,1)S(1)}, u32[]{:S(2)}, u32[]{:S(2)}) collective-permute-start(bf16[13,16,256]{2,1,0:T(8,128)(2,1)S(1)} %get-tuple-element.16), channel_id=1, source_target_pairs={{32,0},{64,32},{96,64},{128,96},{160,128},{192,160},{224,192},{256... | collective-permute-start | bytes 319496 | tf_op jit(solution)/shard_map/ppermute | solution.py:229
  24.5 1.7 %collective-permute-done.1.s_ref = bf16[13,16,256]{2,1,0:T(8,128)(2,1)S(1)} collective-permute-done((bf16[13,16,256]{2,1,0:T(8,128)(2,1)S(1)}, bf16[13,16,256]{2,1,0:T(8,128)(2,1)S(1)}, u32[]{:S(2)}, u32[]{:S(2)}) %collective-permute-start.1) | collective-permute-done | bytes 106528 | tf_op jit(solution)/shard_map/ppermute | solution.py:229
  26.2 0.0 collective-permute-done.n_ref
  26.2 1.0 %band.1 = (bf16[56,16,256]{2,1,0:T(8,128)(2,1)S(1)}, bf16[64,256]{1,0:T(8,128)(2,1)S(1)}, bf16[736,256]{1,0:T(8,128)(2,1)S(1)}, bf16[672,256]{1,0:T(8,128)(2,1)}) custom-call(bf16[33,16,256]{2,1,0:T(8,128)(2,1)S(1)} %get-tuple-element.13.own_ref, bf16[48,256]{1,0:T(8,128)(2,1)S(1)} %get-tuple-element.14.edge_ref, ...), custom_call_target="tpu_custom_call" | custom-call | tf_op jit(solution)/shard_map/band/pallas_call | solution.py:231
  27.2 4.2 %collective-permute-start.2 = (bf16[736,256]{1,0:T(8,128)(2,1)S(1)}, bf16[736,256]{1,0:T(8,128)(2,1)S(1)}, u32[]{:S(2)}, u32[]{:S(2)}) collective-permute-start(bf16[736,256]{1,0:T(8,128)(2,1)S(1)} %get-tuple-element.19), channel_id=1, source_target_pairs={{0,1},{1,2},{2,3},{3,4},{4,5},{5,6},{6,7},{7,8},{8,9},{9,10},{10,1... | collective-permute-start | bytes 1130504 | tf_op jit(solution)/shard_map/ppermute | solution.py:250
  31.3 1.9 %collective-permute-start.3 = (bf16[672,256]{1,0:T(8,128)(2,1)}, bf16[672,256]{1,0:T(8,128)(2,1)S(1)}, u32[]{:S(2)}, u32[]{:S(2)}) collective-permute-start(bf16[672,256]{1,0:T(8,128)(2,1)} %get-tuple-element.20), channel_id=1, source_target_pairs={{0,31},{1,0},{2,1},{3,2},{4,3},{5,4},{6,5},{7,6},{8,7},{9,8},{10,9... | collective-permute-start | bytes 1032200 | tf_op jit(solution)/shard_map/ppermute | solution.py:251
  33.3 0.0 copy-done.4
  33.3 0.0 copy-done.5
  33.3 2.7 %copy.11.w1_ref = bf16[3,3,256,300]{3,2,1,0:T(8,128)(2,1)S(1)} copy(bf16[3,3,256,300]{2,3,1,0:T(8,128)(2,1)} %param.12) | data formatting | bytes 2764800 | tf_op args[4]
  36.0 6.9 %collective-permute-done.3.e_ref = bf16[672,256]{1,0:T(8,128)(2,1)S(1)} collective-permute-done((bf16[672,256]{1,0:T(8,128)(2,1)}, bf16[672,256]{1,0:T(8,128)(2,1)S(1)}, u32[]{:S(2)}, u32[]{:S(2)}) %collective-permute-start.3) | collective-permute-done | bytes 344096 | tf_op jit(solution)/shard_map/ppermute | solution.py:251
  42.9 0.0 collective-permute-done.2.w_ref
  42.9 0.0 copy-start
  42.9 1.6 %copy-done = bf16[3,3,300,300]{3,2,1,0:T(8,128)(2,1)S(1)} copy-done((bf16[3,3,300,300]{3,2,1,0:T(8,128)(2,1)S(1)}, bf16[3,3,300,300]{3,2,1,0:T(8,128)(2,1)}, u32[]{:S(2)}) %copy-start) | copy-done | bytes 1620024
  44.5 9.0 %convolve.1 = f32[32,16,300]{2,1,0:T(8,128)} custom-call(bf16[56,16,256]{2,1,0:T(8,128)(2,1)S(1)} %get-tuple-element.17.band_ref, bf16[64,256]{1,0:T(8,128)(2,1)S(1)} %get-tuple-element.18.col_ref, bf16[736,256]{1,0:T(8,128)(2,1)S(1)} %collective-permute-done.2.w_ref, bf16[672,256]{1,0:T(8,128)(2,1)S(1)} %collective-permute-done.3.e_ref, ...), custom_call_target="tpu_custom_call" | custom-call | tf_op jit(solution)/shard_map/convolve/pallas_call | solution.py:253
  (2 shorter events, 0.0 us)
Async XLA Ops:
  0.0 33.3 %copy-start.4 = (f32[300]{0:T(512)S(1)}, f32[300]{0:T(512)}, u32[]{:S(2)}) copy-start(f32[300]{0:T(512)} %param.13) | copy-start | bytes 3604
  0.0 33.3 %copy-start.5 = (f32[300]{0:T(512)S(1)}, f32[300]{0:T(512)}, u32[]{:S(2)}) copy-start(f32[300]{0:T(512)} %param.15) | copy-start | bytes 3604
  0.8 1.6 %copy-start.1 = (f32[64,32,256]{2,1,0:T(8,128)S(1)}, f32[64,32,256]{2,1,0:T(8,128)}, u32[]{:S(2)}) copy-start(f32[64,32,256]{2,1,0:T(8,128)} %f_ref.1) | copy-start | bytes 6291460
  2.4 0.7 %copy-start.2 = (f32[3,3,256]{2,1,0:T(4,128)S(1)}, f32[3,3,256]{2,1,0:T(4,128)}, u32[]{:S(2)}) copy-start(f32[3,3,256]{2,1,0:T(4,128)} %wd_ref.1) | copy-start | bytes 27652
  3.1 0.7 %copy-start.3 = (f32[256]{0:T(256)S(1)}, f32[256]{0:T(256)}, u32[]{:S(2)}) copy-start(f32[256]{0:T(256)} %param.11) | copy-start | bytes 3076
  9.7 16.5 %collective-permute-start = (bf16[14,16,256]{2,1,0:T(8,128)(2,1)S(1)}, bf16[14,16,256]{2,1,0:T(8,128)(2,1)S(1)}, u32[]{:S(2)}, u32[]{:S(2)}) collective-permute-start(bf16[14,16,256]{2,1,0:T(8,128)(2,1)S(1)} %get-tuple-element.15), channel_id=1, source_target_pairs={{0,32},{32,64},{64,96},{96,128},{128,160},{160,192},{192,224},{224... | collective-permute-start | bytes 344072 | tf_op jit(solution)/shard_map/ppermute | solution.py:228
  13.7 12.5 %collective-permute-start.1 = (bf16[13,16,256]{2,1,0:T(8,128)(2,1)S(1)}, bf16[13,16,256]{2,1,0:T(8,128)(2,1)S(1)}, u32[]{:S(2)}, u32[]{:S(2)}) collective-permute-start(bf16[13,16,256]{2,1,0:T(8,128)(2,1)S(1)} %get-tuple-element.16), channel_id=1, source_target_pairs={{32,0},{64,32},{96,64},{128,96},{160,128},{192,160},{224,192},{256... | collective-permute-start | bytes 319496 | tf_op jit(solution)/shard_map/ppermute | solution.py:229
  27.2 15.8 %collective-permute-start.2 = (bf16[736,256]{1,0:T(8,128)(2,1)S(1)}, bf16[736,256]{1,0:T(8,128)(2,1)S(1)}, u32[]{:S(2)}, u32[]{:S(2)}) collective-permute-start(bf16[736,256]{1,0:T(8,128)(2,1)S(1)} %get-tuple-element.19), channel_id=1, source_target_pairs={{0,1},{1,2},{2,3},{3,4},{4,5},{5,6},{6,7},{7,8},{8,9},{9,10},{10,1... | collective-permute-start | bytes 1130504 | tf_op jit(solution)/shard_map/ppermute | solution.py:250
  31.3 11.6 %collective-permute-start.3 = (bf16[672,256]{1,0:T(8,128)(2,1)}, bf16[672,256]{1,0:T(8,128)(2,1)S(1)}, u32[]{:S(2)}, u32[]{:S(2)}) collective-permute-start(bf16[672,256]{1,0:T(8,128)(2,1)} %get-tuple-element.20), channel_id=1, source_target_pairs={{0,31},{1,0},{2,1},{3,2},{4,3},{5,4},{6,5},{7,6},{8,7},{9,8},{10,9... | collective-permute-start | bytes 1032200 | tf_op jit(solution)/shard_map/ppermute | solution.py:251
  42.9 1.6 %copy-start = (bf16[3,3,300,300]{3,2,1,0:T(8,128)(2,1)S(1)}, bf16[3,3,300,300]{3,2,1,0:T(8,128)(2,1)}, u32[]{:S(2)}) copy-start(bf16[3,3,300,300]{3,2,1,0:T(8,128)(2,1)} %w2_ref.1) | copy-start | bytes 4860004

commit v2 on v0

v2 whole, which is shorter than its diff:
```python
import jax
import jax.numpy as jnp
from jax import lax
from jax.experimental import pallas as pl
from jax.experimental.pallas import tpu as pltpu
from jax.sharding import PartitionSpec as P

ROWS = 32
COLS = 16
HALO = 12
GROUP = 4
SLABS = COLS // GROUP
HALO_SLABS = HALO // GROUP
OWN = ROWS * GROUP
EXT_R = ROWS + 2 * HALO
EXT = EXT_R * GROUP
HID = (ROWS + 16) * GROUP
HID_SLABS = (COLS + 16) // GROUP
EDGE = HALO * GROUP
LANES = 128
CHUNKS = 4
MASKED = 2.0**100
LIMIT = 2.0**90
F32 = jnp.float32
BF16 = jnp.bfloat16


def resolved(x):
    return jnp.where(x > LIMIT, 0.0, x)


def down_kernel(
    f_hbm, ls_hbm, wd_hbm, bd_hbm,
    own_ref, below_ref, edge_ref, keep_ref, pa_ref, pb_ref,
    f_ref, ls_ref, wd_ref, bd_ref, f_sem, sems, mask, patch, edge,
):
    lat = lax.axis_index("lat")
    last = lat == lax.axis_size("lat") - 1
    small = [
        pltpu.make_async_copy(src, dst, sems.at[k])
        for k, (src, dst) in enumerate(((ls_hbm, ls_ref), (wd_hbm, wd_ref), (bd_hbm, bd_ref)))
    ]
    for copy in small:
        copy.start()
    tall = 2 * ROWS // CHUNKS
    copies = {}
    for h in range(2):
        for k in range(CHUNKS):
            copies[h, k] = pltpu.make_async_copy(
                f_hbm.at[pl.ds(k * tall, tall), :, pl.ds(h * LANES, LANES)],
                f_ref.at[h, pl.ds(k * tall, tall)],
                f_sem.at[h, k],
            )
            copies[h, k].start()
    for copy in small:
        copy.wait()

    sea = ls_ref[...].astype(F32)
    for i in range(ROWS):
        mask[COLS * i : COLS * (i + 1)] = jnp.broadcast_to(sea[:, i : i + 1], (COLS, LANES))
    edge[...] = jnp.zeros_like(edge)

    first = lax.broadcasted_iota(jnp.int32, (COLS, LANES), 0) == 0
    holed = jnp.where(first, MASKED, 0.0)
    scale = jnp.where(last, 0.0, 1.0)
    for h in range(2):
        at = slice(h * LANES, (h + 1) * LANES)
        weight = [
            [jnp.broadcast_to(wd_ref[a, b : b + 1, at], (COLS, LANES)) for b in range(3)]
            for a in range(3)
        ]
        bias = jnp.broadcast_to(bd_ref[:, at], (COLS, LANES))
        for i in range(ROWS + 1):
            if i < ROWS and (2 * i) % tall == 0:
                copies[h, 2 * i // tall].wait()
            here, after = None, None
            for a in range(3):
                r = 2 * i - 1 + a
                if r < 0 or r >= 2 * ROWS:
                    continue
                even = f_ref[h, r, pl.ds(0, COLS, stride=2), :]
                odd = f_ref[h, r, pl.ds(1, COLS, stride=2), :]
                p = even * weight[a][1] + odd * weight[a][2]
                q = odd * weight[a][0]
                here = p if here is None else here + p
                after = q if after is None else after + q
            if i == ROWS:
                here, after = here * scale, after * scale
            else:
                here = here + bias
            moved = pltpu.roll(after, 1, 0)
            edge[i : i + 1, at] = moved[0:1]
            value = here + jnp.where(first, 0.0, moved)
            if i == ROWS:
                below_ref[:, at] = value.astype(BF16)
                continue
            kept = mask[COLS * i : COLS * (i + 1)]
            value = jnp.where(kept > 0.5, value, MASKED if i == 0 else holed)
            for q in range(SLABS):
                cells = slice(GROUP * i, GROUP * (i + 1))
                patch[q, cells, at] = value[GROUP * q : GROUP * (q + 1)]
                if h == 0:
                    keep_ref[q, cells] = kept[GROUP * q : GROUP * (q + 1)]

    own_ref[...] = patch[...].astype(BF16)
    edge_ref[...] = edge[...].astype(BF16)

    def write(south_ref, north_ref):
        for q in range(SLABS):
            south_ref[EDGE * q : EDGE * (q + 1)] = own_ref[q, OWN - EDGE : OWN]
            north_ref[EDGE * q : EDGE * (q + 1)] = own_ref[q, 0:EDGE]
        base = EDGE * SLABS
        south_ref[base : base + 16] = below_ref[...]
        south_ref[base + 16 : base + 32] = edge[ROWS - HALO : ROWS - HALO + 16].astype(BF16)
        north_ref[base : base + 16] = edge[0:16].astype(BF16)
        north_ref[base + 16 : base + 32] = jnp.zeros((16, 2 * LANES), BF16)

    even = lax.rem(lat, 2) == 0

    @pl.when(even)
    def _():
        write(pa_ref, pb_ref)

    @pl.when(jnp.logical_not(even))
    def _():
        write(pb_ref, pa_ref)


def band_kernel(
    own_ref, below_ref, edge_ref, ra_ref, rb_ref,
    band_ref, col_ref, pa_ref, pb_ref,
    north, south, tile, col,
):
    even_lat = lax.rem(lax.axis_index("lat"), 2) == 0
    even_lon = lax.rem(lax.axis_index("lon"), 2) == 0

    @pl.when(even_lat)
    def _():
        south[...] = ra_ref[...]
        north[...] = rb_ref[...]

    @pl.when(jnp.logical_not(even_lat))
    def _():
        north[...] = ra_ref[...]
        south[...] = rb_ref[...]

    base = EDGE * SLABS
    col[HALO : HALO + ROWS + 16] = edge_ref[...].astype(F32)
    n_edge = north[base + 16 : base + 32].astype(F32)
    s_edge = south[base : base + 16].astype(F32)
    col[0:HALO] = n_edge[0:HALO]
    col[HALO : HALO + 1] += n_edge[HALO : HALO + 1]
    col[HALO + ROWS : HALO + ROWS + 1] += s_edge[0:1]
    col[HALO + ROWS + 1 : EXT_R] = s_edge[1:HALO]
    col_ref[...] = col[...].astype(BF16)

    above = north[base : base + 16].astype(F32)
    below = below_ref[...].astype(F32)
    for q in range(SLABS):
        cells = slice(GROUP * q, GROUP * (q + 1))
        tile[0, q] = own_ref[q, 0:16].astype(F32)
        tile[1, q] = south[EDGE * q : EDGE * q + 16].astype(F32)
        tile[0, q, 0:GROUP] += above[cells]
        tile[1, q, 0:GROUP] += below[cells]
        top, bottom = tile[0, q], tile[1, q]
        if q > 0:
            top, bottom = resolved(top), resolved(bottom)
        band_ref[q, 0:EDGE] = north[EDGE * q : EDGE * (q + 1)]
        band_ref[q, EDGE : EDGE + 16] = top.astype(BF16)
        band_ref[q, EDGE + 16 : EDGE + OWN] = own_ref[q, 16:OWN]
        band_ref[q, EDGE + OWN : EDGE + OWN + 16] = bottom.astype(BF16)
        band_ref[q, EDGE + OWN + 16 : EXT] = south[EDGE * q + 16 : EDGE * (q + 1)]

    def write(east_ref, west_ref):
        for k in range(HALO_SLABS):
            east_ref[EXT * k : EXT * (k + 1)] = band_ref[SLABS - HALO_SLABS + k]
            west_ref[EXT * k : EXT * (k + 1)] = band_ref[k]
        east_ref[EXT * HALO_SLABS :] = col_ref[...]
        west_ref[EXT * HALO_SLABS :] = jnp.zeros_like(col_ref)

    @pl.when(even_lon)
    def _():
        write(pa_ref, pb_ref)

    @pl.when(jnp.logical_not(even_lon))
    def _():
        write(pb_ref, pa_ref)


def gelu(x):
    return 0.5 * x * (1.0 + lax.erf(x * (0.5**0.5)))


def conv_kernel(
    band_ref, col_ref, ra_ref, rb_ref, keep_ref, w1_ref, b1_ref, w2_hbm, b2_ref,
    out_ref,
    w2_ref, w2_sem, west_col, joined, ext, hidden,
):
    load = pltpu.make_async_copy(w2_hbm, w2_ref, w2_sem)
    load.start()
    lat = lax.axis_index("lat")
    last = lax.axis_size("lat") - 1
    out_ch = b1_ref.shape[1]
    even_lon = lax.rem(lax.axis_index("lon"), 2) == 0
    halves = [slice(h * LANES, (h + 1) * LANES) for h in range(2)]

    def take(w_ref, e_ref):
        for k in range(HALO_SLABS):
            ext[k] = w_ref[EXT * k : EXT * (k + 1)]
            if k > 0:
                ext[HALO_SLABS + SLABS + k] = e_ref[EXT * k : EXT * (k + 1)]
        west_col[...] = w_ref[EXT * HALO_SLABS :].astype(F32)
        for h, at in enumerate(halves):
            joined[1, h] = e_ref[0:EXT, at].astype(F32)

    @pl.when(even_lon)
    def _():
        take(rb_ref, ra_ref)

    @pl.when(jnp.logical_not(even_lon))
    def _():
        take(ra_ref, rb_ref)

    for k in range(1, SLABS):
        ext[HALO_SLABS + k] = band_ref[k]
    firsts = pl.ds(0, EXT_R, stride=GROUP)
    for h, at in enumerate(halves):
        joined[0, h] = band_ref[0, :, at].astype(F32)
        joined[0, h, firsts, :] += west_col[0:EXT_R, at]
        joined[1, h, firsts, :] += col_ref[0:EXT_R, at].astype(F32)
        for side in range(2):
            ext[HALO_SLABS + SLABS * side, :, at] = resolved(joined[side, h]).astype(BF16)

    place = lax.broadcasted_iota(jnp.int32, (HID, 1), 0)
    inside = jnp.logical_and(
        jnp.logical_or(place >= 8 * GROUP, lat > 0),
        jnp.logical_or(place < HID - 8 * GROUP, lat < last),
    )

    def first(k, _):
        total = jnp.zeros((HID, out_ch), F32) + b1_ref[...]
        for a in range(3):
            for b in range(3):
                piece = ext[k + b, 4 * GROUP * a : 4 * GROUP * a + HID]
                total = total + jnp.dot(piece, w1_ref[a, b], preferred_element_type=F32)
        hidden[k] = jnp.where(inside, gelu(total), 0.0).astype(BF16)
        return 0

    lax.fori_loop(0, HID_SLABS, first, 0)
    load.wait()

    for k in range(SLABS):
        total = jnp.zeros((OWN, out_ch), F32) + b2_ref[...]
        for a in range(3):
            for b in range(3):
                piece = hidden[k + 2 * b, 8 * GROUP * a : 8 * GROUP * a + OWN]
                total = total + jnp.dot(piece, w2_ref[a, b], preferred_element_type=F32)
        kept = keep_ref[k]
        kept = jnp.concatenate([kept] * pl.cdiv(out_ch, LANES), axis=1)[:, :out_ch]
        value = (gelu(total) * kept).reshape(ROWS, GROUP, out_ch)
        out_ref[:, GROUP * k : GROUP * (k + 1), :] = value


def partners(axis, start, periodic):
    count = lax.axis_size(axis)
    route = []
    for i in range(start, count, 2):
        j = i + 1
        if j == count and not periodic:
            continue
        route += [(i, j % count), (j % count, i)]
    return route


def in_hbm(array):
    return pltpu.with_memory_space_constraint(array, pltpu.HBM)


def on_device(fields, land_sea, w_depth, b_depth, w_one, b_one, w_two, b_two):
    chans = fields.shape[2]
    out_ch = w_one.shape[3]
    vmem = pl.BlockSpec(memory_space=pltpu.VMEM)
    hbm = pl.BlockSpec(memory_space=pltpu.HBM)

    def shape(*dims, dtype=BF16):
        return jax.ShapeDtypeStruct(dims, dtype)

    lat_rows = SLABS * EDGE + 32
    lon_rows = HALO_SLABS * EXT + 64
    own, below, edge, keep, lat_a, lat_b = pl.pallas_call(
        down_kernel,
        out_shape=(
            shape(SLABS, OWN, chans),
            shape(COLS, chans),
            shape(ROWS + 16, chans),
            shape(SLABS, OWN, LANES, dtype=F32),
            shape(lat_rows, chans),
            shape(lat_rows, chans),
        ),
        in_specs=[hbm] * 4,
        out_specs=[vmem] * 6,
        scratch_shapes=[
            pltpu.VMEM((2, 2 * ROWS, 2 * COLS, LANES), F32),
            pltpu.VMEM((COLS, ROWS), jnp.int32),
            pltpu.VMEM(w_depth.shape, F32),
            pltpu.VMEM((1, chans), F32),
            pltpu.SemaphoreType.DMA((2, CHUNKS)),
            pltpu.SemaphoreType.DMA((3,)),
            pltpu.VMEM((ROWS * COLS, LANES), F32),
            pltpu.VMEM((SLABS, OWN, chans), F32),
            pltpu.VMEM((ROWS + 16, chans), F32),
        ],
        compiler_params=pltpu.CompilerParams(vmem_limit_bytes=16 << 20),
        name="down",
    )(in_hbm(fields), in_hbm(land_sea.T), in_hbm(w_depth), in_hbm(b_depth[None]))

    got_b = lax.ppermute(lat_b, "lat", partners("lat", 1, False))
    got_a = lax.ppermute(lat_a, "lat", partners("lat", 0, False))

    band, col, lon_a, lon_b = pl.pallas_call(
        band_kernel,
        out_shape=(
            shape(SLABS, EXT, chans),
            shape(64, chans),
            shape(lon_rows, chans),
            shape(lon_rows, chans),
        ),
        in_specs=[vmem] * 5,
        out_specs=[vmem] * 4,
        scratch_shapes=[
            pltpu.VMEM((lat_rows, chans), BF16),
            pltpu.VMEM((lat_rows, chans), BF16),
            pltpu.VMEM((2, SLABS, 16, chans), F32),
            pltpu.VMEM((64, chans), F32),
        ],
        compiler_params=pltpu.CompilerParams(vmem_limit_bytes=16 << 20),
        name="band",
    )(own, below, edge, got_a, got_b)

    got_b = lax.ppermute(lon_b, "lon", partners("lon", 1, True))
    got_a = lax.ppermute(lon_a, "lon", partners("lon", 0, True))

    return pl.pallas_call(
        conv_kernel,
        out_shape=shape(ROWS, COLS, out_ch, dtype=F32),
        in_specs=[vmem] * 7 + [hbm, vmem],
        out_specs=vmem,
        scratch_shapes=[
            pltpu.VMEM(w_two.shape, BF16),
            pltpu.SemaphoreType.DMA,
            pltpu.VMEM((64, chans), F32),
            pltpu.VMEM((2, 2, EXT, LANES), F32),
            pltpu.VMEM((2 * HALO_SLABS + SLABS, EXT, chans), BF16),
            pltpu.VMEM((HID_SLABS, HID, out_ch), BF16),
        ],
        compiler_params=pltpu.CompilerParams(vmem_limit_bytes=32 << 20),
        name="convolve",
    )(band, col, got_a, got_b, keep, w_one, b_one[None], in_hbm(w_two), b_two[None])


def solution(mesh):
    return jax.shard_map(
        on_device,
        mesh=mesh,
        in_specs=(P("lat", "lon", None), P("lat", "lon"), P(), P(), P(), P(), P(), P()),
        out_specs=P("lat", "lon", None),
        check_vma=False,
    )
```

time: 97.1 us -> 49.3 us (0.51)
  the two profiles are of different devices: /device:TPU:31 before, /device:TPU:57 now
where the time goes in v2:
time: 49.3 us; the launch traced here: 49 us
  starting transfers between devices  22.4 us (45%)
  Pallas kernels  12 us (24%)
  waiting for transfers between devices  11.9 us (24%)
  local copies, waits for them, and re-layouts  2.69 us (5%)
    ppermute x1, starting transfers between devices, on_device(): got_b = lax.ppermute(lat_b, 'lat', partners('lat', 1, False))  11.1 us
    ppermute x1, waiting for transfers between devices, on_device(): got_b = lax.ppermute(lon_b, 'lon', partners('lon', 1, True))  9.33 us
    pallas_call x1, Pallas kernels, on_device(): pl.pallas_call(conv_kernel, out_shape=shape(ROWS, COLS, out_ch, dtype=F32...  8.79 us
    ppermute x1, starting transfers between devices, on_device(): got_a = lax.ppermute(lat_a, 'lat', partners('lat', 0, False))  4 us
    ppermute x1, starting transfers between devices, on_device(): got_b = lax.ppermute(lon_b, 'lon', partners('lon', 1, True))  3.75 us
    ppermute x1, starting transfers between devices, on_device(): got_a = lax.ppermute(lon_a, 'lon', partners('lon', 0, True))  3.54 us
    unnamed x5, local copies, waits for them, and re-layouts  2.68 us
    ppermute x1, waiting for transfers between devices, on_device(): got_b = lax.ppermute(lat_b, 'lat', partners('lat', 1, False))  2.53 us
  transfers between devices with their start and end apart: 4, of which 2 were waited for; matrix products, arithmetic and copies ran while one was open for 5% of the time, Pallas kernels for 0%

profile of v2, /device:TPU:57, one launch (start us, length us, event | category | flops | bytes accessed | tf_op | source)
XLA Modules:
  0.0 49.0 jit_solution(245062653426181539)
XLA Ops:
  0.0 0.0 copy-start
  0.0 0.0 copy-start.1
  0.0 2.2 %down.1 = (bf16[4,128,256]{2,1,0:T(8,128)(2,1)S(1)}, bf16[16,256]{1,0:T(8,128)(2,1)S(1)}, bf16[48,256]{1,0:T(8,128)(2,1)S(1)}, f32[4,128,128]{2,1,0:T(8,128)S(1)...) custom-call(f32[64,32,256]{2,1,0:T(8,128)} %f_hbm.1, s32[16,32]{1,0:T(8,128)} %bitcast.2, ...), custom_call_target="tpu_custom_call" | custom-call | tf_op jit(solution)/shard_map/down/pallas_call | solution.py:290
  2.2 4.0 %collective-permute-start = (bf16[224,256]{1,0:T(8,128)(2,1)S(1)}, bf16[224,256]{1,0:T(8,128)(2,1)S(1)}, u32[]{:S(2)}, u32[]{:S(2)}) collective-permute-start(bf16[224,256]{1,0:T(8,128)(2,1)S(1)} %get-tuple-element.18), channel_id=1, source_target_pairs={{0,32},{32,0},{64,96},{96,64},{128,160},{160,128},{192,224},{224,1... | collective-permute-start | bytes 344072 | tf_op jit(solution)/shard_map/ppermute | solution.py:318
  6.2 11.1 %collective-permute-start.1 = (bf16[224,256]{1,0:T(8,128)(2,1)S(1)}, bf16[224,256]{1,0:T(8,128)(2,1)S(1)}, u32[]{:S(2)}, u32[]{:S(2)}) collective-permute-start(bf16[224,256]{1,0:T(8,128)(2,1)S(1)} %get-tuple-element.19), channel_id=1, source_target_pairs={{32,64},{64,32},{96,128},{128,96},{160,192},{192,160},{224,256},{2... | collective-permute-start | bytes 344072 | tf_op jit(solution)/shard_map/ppermute | solution.py:317
  17.3 0.0 collective-permute-done.ra_ref
  17.3 2.5 %collective-permute-done.1.rb_ref = bf16[224,256]{1,0:T(8,128)(2,1)S(1)} collective-permute-done((bf16[224,256]{1,0:T(8,128)(2,1)S(1)}, bf16[224,256]{1,0:T(8,128)(2,1)S(1)}, u32[]{:S(2)}, u32[]{:S(2)}) %collective-permute-start.1) | collective-permute-done | bytes 114720 | tf_op jit(solution)/shard_map/ppermute | solution.py:317
  19.8 1.0 %band.1 = (bf16[4,224,256]{2,1,0:T(8,128)(2,1)S(1)}, bf16[64,256]{1,0:T(8,128)(2,1)S(1)}, bf16[736,256]{1,0:T(8,128)(2,1)}, bf16[736,256]{1,0:T(8,128)(2,1)}) custom-call(bf16[4,128,256]{2,1,0:T(8,128)(2,1)S(1)} %get-tuple-element.15.own_ref, bf16[16,256]{1,0:T(8,128)(2,1)S(1)} %get-tuple-element.16.below_ref, ...), custom_call_target="tpu_custom_call" | custom-call | tf_op jit(solution)/shard_map/band/pallas_call | solution.py:320
  20.8 3.5 %collective-permute-start.2 = (bf16[736,256]{1,0:T(8,128)(2,1)}, bf16[736,256]{1,0:T(8,128)(2,1)S(1)}, u32[]{:S(2)}, u32[]{:S(2)}) collective-permute-start(bf16[736,256]{1,0:T(8,128)(2,1)} %get-tuple-element.22), channel_id=1, source_target_pairs={{0,1},{1,0},{2,3},{3,2},{4,5},{5,4},{6,7},{7,6},{8,9},{9,8},{10,11... | collective-permute-start | bytes 1130504 | tf_op jit(solution)/shard_map/ppermute | solution.py:341
  24.4 3.7 %collective-permute-start.3 = (bf16[736,256]{1,0:T(8,128)(2,1)}, bf16[736,256]{1,0:T(8,128)(2,1)S(1)}, u32[]{:S(2)}, u32[]{:S(2)}) collective-permute-start(bf16[736,256]{1,0:T(8,128)(2,1)} %get-tuple-element.23), channel_id=1, source_target_pairs={{1,2},{2,1},{3,4},{4,3},{5,6},{6,5},{7,8},{8,7},{9,10},{10,9},{11,... | collective-permute-start | bytes 1130504 | tf_op jit(solution)/shard_map/ppermute | solution.py:340
  28.1 0.0 copy-done
  28.1 0.0 copy-done.1
  28.2 2.7 %copy.9.w1_ref = bf16[3,3,256,300]{3,2,1,0:T(8,128)(2,1)S(1)} copy(bf16[3,3,256,300]{2,3,1,0:T(8,128)(2,1)} %param.12) | data formatting | bytes 2764800 | tf_op args[4]
  30.9 0.0 collective-permute-done.2.ra_ref
  30.9 9.3 %collective-permute-done.3.rb_ref = bf16[736,256]{1,0:T(8,128)(2,1)S(1)} collective-permute-done((bf16[736,256]{1,0:T(8,128)(2,1)}, bf16[736,256]{1,0:T(8,128)(2,1)S(1)}, u32[]{:S(2)}, u32[]{:S(2)}) %collective-permute-start.3) | collective-permute-done | bytes 376864 | tf_op jit(solution)/shard_map/ppermute | solution.py:340
  40.2 8.8 %convolve.1 = f32[32,16,300]{2,1,0:T(8,128)} custom-call(bf16[4,224,256]{2,1,0:T(8,128)(2,1)S(1)} %get-tuple-element.20.band_ref, bf16[64,256]{1,0:T(8,128)(2,1)S(1)} %get-tuple-element.21.col_ref, bf16[736,256]{1,0:T(8,128)(2,1)S(1)} %collective-permute-done.2.ra_ref, bf16[736,256]{1,0:T(8,128)(2,1)S(1)} %collective-permute-done.3.rb_ref, ...), custom_call_target="tpu_custom_call" | custom-call | tf_op jit(solution)/shard_map/convolve/pallas_call | solution.py:343
  (2 shorter events, 0.0 us)
Async XLA Ops:
  0.0 28.1 %copy-start = (f32[300]{0:T(512)S(1)}, f32[300]{0:T(512)}, u32[]{:S(2)}) copy-start(f32[300]{0:T(512)} %param.13) | copy-start | bytes 3604
  0.0 28.1 %copy-start.1 = (f32[300]{0:T(512)S(1)}, f32[300]{0:T(512)}, u32[]{:S(2)}) copy-start(f32[300]{0:T(512)} %param.15) | copy-start | bytes 3604
  2.2 15.1 %collective-permute-start = (bf16[224,256]{1,0:T(8,128)(2,1)S(1)}, bf16[224,256]{1,0:T(8,128)(2,1)S(1)}, u32[]{:S(2)}, u32[]{:S(2)}) collective-permute-start(bf16[224,256]{1,0:T(8,128)(2,1)S(1)} %get-tuple-element.18), channel_id=1, source_target_pairs={{0,32},{32,0},{64,96},{96,64},{128,160},{160,128},{192,224},{224,1... | collective-permute-start | bytes 344072 | tf_op jit(solution)/shard_map/ppermute | solution.py:318
  6.2 13.6 %collective-permute-start.1 = (bf16[224,256]{1,0:T(8,128)(2,1)S(1)}, bf16[224,256]{1,0:T(8,128)(2,1)S(1)}, u32[]{:S(2)}, u32[]{:S(2)}) collective-permute-start(bf16[224,256]{1,0:T(8,128)(2,1)S(1)} %get-tuple-element.19), channel_id=1, source_target_pairs={{32,64},{64,32},{96,128},{128,96},{160,192},{192,160},{224,256},{2... | collective-permute-start | bytes 344072 | tf_op jit(solution)/shard_map/ppermute | solution.py:317
  20.8 10.0 %collective-permute-start.2 = (bf16[736,256]{1,0:T(8,128)(2,1)}, bf16[736,256]{1,0:T(8,128)(2,1)S(1)}, u32[]{:S(2)}, u32[]{:S(2)}) collective-permute-start(bf16[736,256]{1,0:T(8,128)(2,1)} %get-tuple-element.22), channel_id=1, source_target_pairs={{0,1},{1,0},{2,3},{3,2},{4,5},{5,4},{6,7},{7,6},{8,9},{9,8},{10,11... | collective-permute-start | bytes 1130504 | tf_op jit(solution)/shard_map/ppermute | solution.py:341
  24.4 15.8 %collective-permute-start.3 = (bf16[736,256]{1,0:T(8,128)(2,1)}, bf16[736,256]{1,0:T(8,128)(2,1)S(1)}, u32[]{:S(2)}, u32[]{:S(2)}) collective-permute-start(bf16[736,256]{1,0:T(8,128)(2,1)} %get-tuple-element.23), channel_id=1, source_target_pairs={{1,2},{2,1},{3,4},{4,3},{5,6},{6,5},{7,8},{8,7},{9,10},{10,9},{11,... | collective-permute-start | bytes 1130504 | tf_op jit(solution)/shard_map/ppermute | solution.py:340

commit v3 on v2

--- a/solution.py
+++ b/solution.py
@@ -15,7 +15,7 @@
 EXT_R = ROWS + 2 * HALO
 EXT = EXT_R * GROUP
 HID = (ROWS + 16) * GROUP
-HID_SLABS = (COLS + 16) // GROUP
+SIDE = (COLS + 16) // GROUP // 2
 EDGE = HALO * GROUP
 LANES = 128
 CHUNKS = 4
@@ -127,7 +127,7 @@
 
 
 def band_kernel(
-    own_ref, below_ref, edge_ref, ra_ref, rb_ref,
+    own_ref, below_ref, edge_ref, rb_ref, ra_ref,
     band_ref, col_ref, pa_ref, pb_ref,
     north, south, tile, col,
 ):
@@ -191,73 +191,109 @@
     return 0.5 * x * (1.0 + lax.erf(x * (0.5**0.5)))
 
 
-def conv_kernel(
-    band_ref, col_ref, ra_ref, rb_ref, keep_ref, w1_ref, b1_ref, w2_hbm, b2_ref,
-    out_ref,
-    w2_ref, w2_sem, west_col, joined, ext, hidden,
+def half_sums(
+    side_west, band_ref, col_ref, far_ref, w1_ref, b1_ref, w2_ref, load, sums,
+    west_col, joined, ext, hidden,
 ):
-    load = pltpu.make_async_copy(w2_hbm, w2_ref, w2_sem)
-    load.start()
     lat = lax.axis_index("lat")
     last = lax.axis_size("lat") - 1
     out_ch = b1_ref.shape[1]
-    even_lon = lax.rem(lax.axis_index("lon"), 2) == 0
+    side_east = jnp.logical_not(side_west)
     halves = [slice(h * LANES, (h + 1) * LANES) for h in range(2)]
-
-    def take(w_ref, e_ref):
+    firsts = pl.ds(0, EXT_R, stride=GROUP)
+
+    @pl.when(side_west)
+    def _():
+        west_col[...] = far_ref[EXT * HALO_SLABS :].astype(F32)
         for k in range(HALO_SLABS):
-            ext[k] = w_ref[EXT * k : EXT * (k + 1)]
-            if k > 0:
-                ext[HALO_SLABS + SLABS + k] = e_ref[EXT * k : EXT * (k + 1)]
-        west_col[...] = w_ref[EXT * HALO_SLABS :].astype(F32)
+            ext[k] = far_ref[EXT * k : EXT * (k + 1)]
+        for k in range(1, HALO_SLABS):
+            ext[HALO_SLABS + k] = band_ref[k]
         for h, at in enumerate(halves):
-            joined[1, h] = e_ref[0:EXT, at].astype(F32)
-
-    @pl.when(even_lon)
-    def _():
-        take(rb_ref, ra_ref)
-
-    @pl.when(jnp.logical_not(even_lon))
-    def _():
-        take(ra_ref, rb_ref)
-
-    for k in range(1, SLABS):
-        ext[HALO_SLABS + k] = band_ref[k]
-    firsts = pl.ds(0, EXT_R, stride=GROUP)
+            joined[h] = band_ref[0, :, at].astype(F32)
+
+    @pl.when(side_east)
+    def _():
+        west_col[...] = col_ref[...].astype(F32)
+        for k in range(1, HALO_SLABS):
+            ext[HALO_SLABS + k] = far_ref[EXT * k : EXT * (k + 1)]
+        for k in range(HALO_SLABS):
+            ext[k] = band_ref[k + 1]
+        for h, at in enumerate(halves):
+            joined[h] = far_ref[0:EXT, at].astype(F32)
+
     for h, at in enumerate(halves):
-        joined[0, h] = band_ref[0, :, at].astype(F32)
-        joined[0, h, firsts, :] += west_col[0:EXT_R, at]
-        joined[1, h, firsts, :] += col_ref[0:EXT_R, at].astype(F32)
-        for side in range(2):
-            ext[HALO_SLABS + SLABS * side, :, at] = resolved(joined[side, h]).astype(BF16)
+        joined[h, firsts, :] += west_col[0:EXT_R, at]
+        ext[HALO_SLABS, :, at] = resolved(joined[h]).astype(BF16)
 
     place = lax.broadcasted_iota(jnp.int32, (HID, 1), 0)
     inside = jnp.logical_and(
         jnp.logical_or(place >= 8 * GROUP, lat > 0),
         jnp.logical_or(place < HID - 8 * GROUP, lat < last),
     )
-
-    def first(k, _):
+    for k in range(SIDE):
         total = jnp.zeros((HID, out_ch), F32) + b1_ref[...]
         for a in range(3):
             for b in range(3):
                 piece = ext[k + b, 4 * GROUP * a : 4 * GROUP * a + HID]
                 total = total + jnp.dot(piece, w1_ref[a, b], preferred_element_type=F32)
         hidden[k] = jnp.where(inside, gelu(total), 0.0).astype(BF16)
-        return 0
-
-    lax.fori_loop(0, HID_SLABS, first, 0)
     load.wait()
 
+    def second(first_slab):
+        for k in range(SLABS):
+            total = sums[k]
+            for b in range(3):
+                slab = k + 2 * b - first_slab
+                if slab < 0 or slab >= SIDE:
+                    continue
+                for a in range(3):
+                    piece = hidden[slab, 8 * GROUP * a : 8 * GROUP * a + OWN]
+                    total = total + jnp.dot(piece, w2_ref[a, b], preferred_element_type=F32)
+            sums[k] = total
+
+    @pl.when(side_west)
+    def _():
+        second(0)
+
+    @pl.when(side_east)
+    def _():
+        second(SIDE)
+
+
+def near_kernel(
+    band_ref, col_ref, far_ref, w1_ref, b1_ref, w2_hbm, b2_ref,
+    sums_ref,
+    w2_ref, w2_sem, west_col, joined, ext, hidden,
+):
+    load = pltpu.make_async_copy(w2_hbm, w2_ref, w2_sem)
+    load.start()
+    sums_ref[...] = jnp.broadcast_to(b2_ref[...], sums_ref.shape)
+    odd = lax.rem(lax.axis_index("lon"), 2) == 1
+    half_sums(
+        odd, band_ref, col_ref, far_ref, w1_ref, b1_ref, w2_ref, load, sums_ref,
+        west_col, joined, ext, hidden,
+    )
+
+
+def far_kernel(
+    band_ref, col_ref, far_ref, w1_ref, b1_ref, w2_hbm, near_ref, keep_ref,
+    out_ref,
+    w2_ref, w2_sem, west_col, joined, ext, hidden, sums,
+):
+    load = pltpu.make_async_copy(w2_hbm, w2_ref, w2_sem)
+    load.start()
+    out_ch = b1_ref.shape[1]
+    sums[...] = near_ref[...]
+    even = lax.rem(lax.axis_index("lon"), 2) == 0
+    half_sums(
+        even, band_ref, col_ref, far_ref, w1_ref, b1_ref, w2_ref, load, sums,
+        west_col, joined, ext, hidden,
+    )
     for k in range(SLABS):
-        total = jnp.zeros((OWN, out_ch), F32) + b2_ref[...]
-        for a in range(3):
-            for b in range(3):
-                piece = hidden[k + 2 * b, 8 * GROUP * a : 8 * GROUP * a + OWN]
-                total = total + jnp.dot(piece, w2_ref[a, b], preferred_element_type=F32)
         kept = keep_ref[k]
         kept = jnp.concatenate([kept] * pl.cdiv(out_ch, LANES), axis=1)[:, :out_ch]
-        value = (gelu(total) * kept).reshape(ROWS, GROUP, out_ch)
+        value = (gelu(sums[k]) * kept).reshape(ROWS, GROUP, out_ch)
         out_ref[:, GROUP * k : GROUP * (k + 1), :] = value
 
 
@@ -310,7 +346,7 @@
             pltpu.VMEM((SLABS, OWN, chans), F32),
             pltpu.VMEM((ROWS + 16, chans), F32),
         ],
-        compiler_params=pltpu.CompilerParams(vmem_limit_bytes=16 << 20),
+        compiler_params=pltpu.CompilerParams(vmem_limit_bytes=10 << 20),
         name="down",
     )(in_hbm(fields), in_hbm(land_sea.T), in_hbm(w_depth), in_hbm(b_depth[None]))
 
@@ -333,29 +369,45 @@
             pltpu.VMEM((2, SLABS, 16, chans), F32),
             pltpu.VMEM((64, chans), F32),
         ],
-        compiler_params=pltpu.CompilerParams(vmem_limit_bytes=16 << 20),
+        compiler_params=pltpu.CompilerParams(vmem_limit_bytes=10 << 20),
         name="band",
-    )(own, below, edge, got_a, got_b)
+    )(own, below, edge, got_b, got_a)
 
     got_b = lax.ppermute(lon_b, "lon", partners("lon", 1, True))
     got_a = lax.ppermute(lon_a, "lon", partners("lon", 0, True))
 
+    scratch = [
+        pltpu.VMEM(w_two.shape, BF16),
+        pltpu.SemaphoreType.DMA,
+        pltpu.VMEM((64, chans), F32),
+        pltpu.VMEM((2, EXT, LANES), F32),
+        pltpu.VMEM((2 * HALO_SLABS, EXT, chans), BF16),
+        pltpu.VMEM((SIDE, HID, out_ch), BF16),
+    ]
+    w_two, b_one = in_hbm(w_two), b_one[None]
+    flops = 2 * SIDE * HID * 9 * chans * out_ch + 2 * 6 * OWN * 3 * out_ch * out_ch
+    cost = pl.CostEstimate(flops=flops, bytes_accessed=4 << 20, transcendentals=SIDE * HID * out_ch)
+    near = pl.pallas_call(
+        near_kernel,
+        out_shape=shape(SLABS, OWN, out_ch, dtype=F32),
+        in_specs=[vmem] * 5 + [hbm, vmem],
+        out_specs=vmem,
+        scratch_shapes=scratch,
+        compiler_params=pltpu.CompilerParams(vmem_limit_bytes=14 << 20),
+        cost_estimate=cost,
+        name="near_half",
+    )(band, col, got_a, w_one, b_one, w_two, b_two[None])
+
     return pl.pallas_call(
-        conv_kernel,
+        far_kernel,
         out_shape=shape(ROWS, COLS, out_ch, dtype=F32),
-        in_specs=[vmem] * 7 + [hbm, vmem],
+        in_specs=[vmem] * 5 + [hbm, vmem, vmem],
         out_specs=vmem,
-        scratch_shapes=[
-            pltpu.VMEM(w_two.shape, BF16),
-            pltpu.SemaphoreType.DMA,
-            pltpu.VMEM((64, chans), F32),
-            pltpu.VMEM((2, 2, EXT, LANES), F32),
-            pltpu.VMEM((2 * HALO_SLABS + SLABS, EXT, chans), BF16),
-            pltpu.VMEM((HID_SLABS, HID, out_ch), BF16),
-        ],
-        compiler_params=pltpu.CompilerParams(vmem_limit_bytes=32 << 20),
-        name="convolve",
-    )(band, col, got_a, got_b, keep, w_one, b_one[None], in_hbm(w_two), b_two[None])
+        scratch_shapes=scratch + [pltpu.VMEM((SLABS, OWN, out_ch), F32)],
+        compiler_params=pltpu.CompilerParams(vmem_limit_bytes=14 << 20),
+        cost_estimate=cost,
+        name="far_half",
+    )(band, col, got_b, w_one, b_one, w_two, near, keep)
 
 
 def solution(mesh):

time: 49.3 us -> 43.9 us (0.89)
  waiting for transfers between devices: 11.9 us -> 8 us
  starting transfers between devices: 22.4 us -> 21.5 us
  Pallas kernels: 12 us -> 11.4 us
    ppermute x1, waiting for transfers between devices: 9.33 us -> 4.39 us  [on_device(): got_b = lax.ppermute(lon_b, 'lon', partners('lon', 1, True))]
    ppermute x1, waiting for transfers between devices: 0.01 us -> 2.68 us  [on_device(): got_a = lax.ppermute(lat_a, 'lat', partners('lat', 0, False))]
    ppermute x1, starting transfers between devices: 4 us -> 1.92 us  [on_device(): got_a = lax.ppermute(lat_a, 'lat', partners('lat', 0, False))]
    ppermute x1, starting transfers between devices: 11.1 us -> 12.9 us  [on_device(): got_b = lax.ppermute(lat_b, 'lat', partners('lat', 1, False))]
    ppermute x1, waiting for transfers between devices: 2.53 us -> 0.93 us  [on_device(): got_b = lax.ppermute(lat_b, 'lat', partners('lat', 1, False))]
    ppermute x1, starting transfers between devices: 3.75 us -> 2.67 us  [on_device(): got_b = lax.ppermute(lon_b, 'lon', partners('lon', 1, True))]
    pallas_call x1 -> x2, Pallas kernels: 8.79 us -> 8.2 us  [the longest x1 4.67 us: on_device(): pl.pallas_call(far_kernel, out_shape=shape(ROWS, COLS, out_ch, dtype=F32)...]
  transfers between devices with their start and end apart: 4 -> 4, of which waited for: 2 -> 3; matrix products, arithmetic and copies ran while one was open for 5% -> 6% of each run, Pallas kernels for 0% -> 8%
where the time goes in v3:
time: 43.9 us; the launch traced here: 43.7 us
  starting transfers between devices  21.5 us (49%)
  Pallas kernels  11.4 us (26%)
  waiting for transfers between devices  8 us (18%)
  local copies, waits for them, and re-layouts  2.69 us (6%)
    ppermute x1, starting transfers between devices, on_device(): got_b = lax.ppermute(lat_b, 'lat', partners('lat', 1, False))  12.9 us
    pallas_call x1, Pallas kernels, on_device(): pl.pallas_call(far_kernel, out_shape=shape(ROWS, COLS, out_ch, dtype=F32)...  4.67 us
    ppermute x1, waiting for transfers between devices, on_device(): got_b = lax.ppermute(lon_b, 'lon', partners('lon', 1, True))  4.39 us
    ppermute x1, starting transfers between devices, on_device(): got_a = lax.ppermute(lon_a, 'lon', partners('lon', 0, True))  4 us
    pallas_call x1, Pallas kernels, on_device(): pl.pallas_call(near_kernel, out_shape=shape(SLABS, OWN, out_ch, dtype=F32...  3.53 us
    unnamed x5, local copies, waits for them, and re-layouts  2.68 us
    ppermute x1, waiting for transfers between devices, on_device(): got_a = lax.ppermute(lat_a, 'lat', partners('lat', 0, False))  2.68 us
    ppermute x1, starting transfers between devices, on_device(): got_b = lax.ppermute(lon_b, 'lon', partners('lon', 1, True))  2.67 us
  transfers between devices with their start and end apart: 4, of which 3 were waited for; matrix products, arithmetic and copies ran while one was open for 6% of the time, Pallas kernels for 8%

profile of v3, /device:TPU:57, one launch (start us, length us, event | category | flops | bytes accessed | tf_op | source)
XLA Modules:
  0.0 43.7 jit_solution(1816650261481262429)
XLA Ops:
  0.0 0.0 copy-start
  0.0 0.0 copy-start.1
  0.0 2.2 %down.1 = (bf16[4,128,256]{2,1,0:T(8,128)(2,1)S(1)}, bf16[16,256]{1,0:T(8,128)(2,1)S(1)}, bf16[48,256]{1,0:T(8,128)(2,1)S(1)}, f32[4,128,128]{2,1,0:T(8,128)S(1)...) custom-call(f32[64,32,256]{2,1,0:T(8,128)} %f_hbm.1, s32[16,32]{1,0:T(8,128)} %bitcast.2, ...), custom_call_target="tpu_custom_call" | custom-call | tf_op jit(solution)/shard_map/down/pallas_call | solution.py:326
  2.2 12.9 %collective-permute-start = (bf16[224,256]{1,0:T(8,128)(2,1)S(1)}, bf16[224,256]{1,0:T(8,128)(2,1)S(1)}, u32[]{:S(2)}, u32[]{:S(2)}) collective-permute-start(bf16[224,256]{1,0:T(8,128)(2,1)S(1)} %get-tuple-element.18), channel_id=1, source_target_pairs={{32,64},{64,32},{96,128},{128,96},{160,192},{192,160},{224,256},{2... | collective-permute-start | bytes 344072 | tf_op jit(solution)/shard_map/ppermute | solution.py:353
  15.1 1.9 %collective-permute-start.1 = (bf16[224,256]{1,0:T(8,128)(2,1)S(1)}, bf16[224,256]{1,0:T(8,128)(2,1)S(1)}, u32[]{:S(2)}, u32[]{:S(2)}) collective-permute-start(bf16[224,256]{1,0:T(8,128)(2,1)S(1)} %get-tuple-element.19), channel_id=1, source_target_pairs={{0,32},{32,0},{64,96},{96,64},{128,160},{160,128},{192,224},{224,1... | collective-permute-start | bytes 344072 | tf_op jit(solution)/shard_map/ppermute | solution.py:354
  17.0 0.9 %collective-permute-done.rb_ref = bf16[224,256]{1,0:T(8,128)(2,1)S(1)} collective-permute-done((bf16[224,256]{1,0:T(8,128)(2,1)S(1)}, bf16[224,256]{1,0:T(8,128)(2,1)S(1)}, u32[]{:S(2)}, u32[]{:S(2)}) %collective-permute-start) | collective-permute-done | bytes 114720 | tf_op jit(solution)/shard_map/ppermute | solution.py:353
  18.0 2.7 %collective-permute-done.1.ra_ref = bf16[224,256]{1,0:T(8,128)(2,1)S(1)} collective-permute-done((bf16[224,256]{1,0:T(8,128)(2,1)S(1)}, bf16[224,256]{1,0:T(8,128)(2,1)S(1)}, u32[]{:S(2)}, u32[]{:S(2)}) %collective-permute-start.1) | collective-permute-done | bytes 114720 | tf_op jit(solution)/shard_map/ppermute | solution.py:354
  20.6 1.0 %band.1 = (bf16[4,224,256]{2,1,0:T(8,128)(2,1)S(1)}, bf16[64,256]{1,0:T(8,128)(2,1)S(1)}, bf16[736,256]{1,0:T(8,128)(2,1)}, bf16[736,256]{1,0:T(8,128)(2,1)}) custom-call(bf16[4,128,256]{2,1,0:T(8,128)(2,1)S(1)} %get-tuple-element.15.own_ref, bf16[16,256]{1,0:T(8,128)(2,1)S(1)} %get-tuple-element.16.below_ref, ...), custom_call_target="tpu_custom_call" | custom-call | tf_op jit(solution)/shard_map/band/pallas_call | solution.py:356
  21.6 4.0 %collective-permute-start.3 = (bf16[736,256]{1,0:T(8,128)(2,1)}, bf16[736,256]{1,0:T(8,128)(2,1)S(1)}, u32[]{:S(2)}, u32[]{:S(2)}) collective-permute-start(bf16[736,256]{1,0:T(8,128)(2,1)} %get-tuple-element.23), channel_id=1, source_target_pairs={{0,1},{1,0},{2,3},{3,2},{4,5},{5,4},{6,7},{7,6},{8,9},{9,8},{10,11... | collective-permute-start | bytes 1130504 | tf_op jit(solution)/shard_map/ppermute | solution.py:377
  25.6 2.7 %collective-permute-start.2 = (bf16[736,256]{1,0:T(8,128)(2,1)}, bf16[736,256]{1,0:T(8,128)(2,1)S(1)}, u32[]{:S(2)}, u32[]{:S(2)}) collective-permute-start(bf16[736,256]{1,0:T(8,128)(2,1)} %get-tuple-element.22), channel_id=1, source_target_pairs={{1,2},{2,1},{3,4},{4,3},{5,6},{6,5},{7,8},{8,7},{9,10},{10,9},{11,... | collective-permute-start | bytes 1130504 | tf_op jit(solution)/shard_map/ppermute | solution.py:376
  28.3 0.0 copy-done
  28.3 0.0 copy-done.1
  28.4 2.7 %copy.10.w1_ref = bf16[3,3,256,300]{3,2,1,0:T(8,128)(2,1)S(1)} copy(bf16[3,3,256,300]{2,3,1,0:T(8,128)(2,1)} %param.12) | data formatting | bytes 2764800 | tf_op args[4]
  31.0 0.0 collective-permute-done.3.far_ref
  31.1 3.5 %near_half.1.near_ref = f32[4,128,300]{2,1,0:T(8,128)S(1)} custom-call(bf16[4,224,256]{2,1,0:T(8,128)(2,1)S(1)} %get-tuple-element.20.band_ref, bf16[64,256]{1,0:T(8,128)(2,1)S(1)} %get-tuple-element.21.col_ref, bf16[736,256]{1,0:T(8,128)(2,1)S(1)} %collective-permute-done.3.far_ref, bf16[3,3,256,300]{3,2,1,0:T(8,128)(2,1)S(1)} %copy.10.w1_ref, ...), custom_call_target="tpu_custom_call" | custom-call | flops 1476403200 | bytes 4194304 | tf_op jit(solution)/shard_map/near_half/pallas_call | solution.py:390
  34.6 4.4 %collective-permute-done.2.far_ref = bf16[736,256]{1,0:T(8,128)(2,1)S(1)} collective-permute-done((bf16[736,256]{1,0:T(8,128)(2,1)}, bf16[736,256]{1,0:T(8,128)(2,1)S(1)}, u32[]{:S(2)}, u32[]{:S(2)}) %collective-permute-start.2) | collective-permute-done | bytes 376864 | tf_op jit(solution)/shard_map/ppermute | solution.py:376
  39.0 4.7 %far_half.1 = f32[32,16,300]{2,1,0:T(8,128)} custom-call(bf16[4,224,256]{2,1,0:T(8,128)(2,1)S(1)} %get-tuple-element.20.band_ref, bf16[64,256]{1,0:T(8,128)(2,1)S(1)} %get-tuple-element.21.col_ref, bf16[736,256]{1,0:T(8,128)(2,1)S(1)} %collective-permute-done.2.far_ref, bf16[3,3,256,300]{3,2,1,0:T(8,128)(2,1)S(1)} %copy.10.w1_ref, ...), custom_call_target="tpu_custom_call" | custom-call | flops 1476403200 | bytes 4194304 | tf_op jit(solution)/shard_map/far_half/pallas_call | solution.py:401
  (2 shorter events, 0.0 us)
Async XLA Ops:
  0.0 28.3 %copy-start = (f32[300]{0:T(512)S(1)}, f32[300]{0:T(512)}, u32[]{:S(2)}) copy-start(f32[300]{0:T(512)} %param.13) | copy-start | bytes 3604
  0.0 28.3 %copy-start.1 = (f32[300]{0:T(512)S(1)}, f32[300]{0:T(512)}, u32[]{:S(2)}) copy-start(f32[300]{0:T(512)} %param.15) | copy-start | bytes 3604
  2.2 15.8 %collective-permute-start = (bf16[224,256]{1,0:T(8,128)(2,1)S(1)}, bf16[224,256]{1,0:T(8,128)(2,1)S(1)}, u32[]{:S(2)}, u32[]{:S(2)}) collective-permute-start(bf16[224,256]{1,0:T(8,128)(2,1)S(1)} %get-tuple-element.18), channel_id=1, source_target_pairs={{32,64},{64,32},{96,128},{128,96},{160,192},{192,160},{224,256},{2... | collective-permute-start | bytes 344072 | tf_op jit(solution)/shard_map/ppermute | solution.py:353
  15.1 5.5 %collective-permute-start.1 = (bf16[224,256]{1,0:T(8,128)(2,1)S(1)}, bf16[224,256]{1,0:T(8,128)(2,1)S(1)}, u32[]{:S(2)}, u32[]{:S(2)}) collective-permute-start(bf16[224,256]{1,0:T(8,128)(2,1)S(1)} %get-tuple-element.19), channel_id=1, source_target_pairs={{0,32},{32,0},{64,96},{96,64},{128,160},{160,128},{192,224},{224,1... | collective-permute-start | bytes 344072 | tf_op jit(solution)/shard_map/ppermute | solution.py:354
  21.6 9.4 %collective-permute-start.3 = (bf16[736,256]{1,0:T(8,128)(2,1)}, bf16[736,256]{1,0:T(8,128)(2,1)S(1)}, u32[]{:S(2)}, u32[]{:S(2)}) collective-permute-start(bf16[736,256]{1,0:T(8,128)(2,1)} %get-tuple-element.23), channel_id=1, source_target_pairs={{0,1},{1,0},{2,3},{3,2},{4,5},{5,4},{6,7},{7,6},{8,9},{9,8},{10,11... | collective-permute-start | bytes 1130504 | tf_op jit(solution)/shard_map/ppermute | solution.py:377
  25.6 13.4 %collective-permute-start.2 = (bf16[736,256]{1,0:T(8,128)(2,1)}, bf16[736,256]{1,0:T(8,128)(2,1)S(1)}, u32[]{:S(2)}, u32[]{:S(2)}) collective-permute-start(bf16[736,256]{1,0:T(8,128)(2,1)} %get-tuple-element.22), channel_id=1, source_target_pairs={{1,2},{2,1},{3,4},{4,3},{5,6},{6,5},{7,8},{8,7},{9,10},{10,9},{11,... | collective-permute-start | bytes 1130504 | tf_op jit(solution)/shard_map/ppermute | solution.py:376

commit v4 on v3

--- a/solution.py
+++ b/solution.py
@@ -2,6 +2,7 @@
 import jax.numpy as jnp
 from jax import lax
 from jax.experimental import pallas as pl
+from jax.experimental.layout import Layout, with_layout_constraint
 from jax.experimental.pallas import tpu as pltpu
 from jax.sharding import PartitionSpec as P
 
@@ -31,7 +32,7 @@
 
 def down_kernel(
     f_hbm, ls_hbm, wd_hbm, bd_hbm,
-    own_ref, below_ref, edge_ref, keep_ref, pa_ref, pb_ref,
+    own_ref, below_ref, edge_ref, keep_ref, south_ref, pa_ref, north_ref,
     f_ref, ls_ref, wd_ref, bd_ref, f_sem, sems, mask, patch, edge,
 ):
     lat = lax.axis_index("lat")
@@ -105,29 +106,28 @@
     own_ref[...] = patch[...].astype(BF16)
     edge_ref[...] = edge[...].astype(BF16)
 
-    def write(south_ref, north_ref):
-        for q in range(SLABS):
-            south_ref[EDGE * q : EDGE * (q + 1)] = own_ref[q, OWN - EDGE : OWN]
-            north_ref[EDGE * q : EDGE * (q + 1)] = own_ref[q, 0:EDGE]
-        base = EDGE * SLABS
-        south_ref[base : base + 16] = below_ref[...]
-        south_ref[base + 16 : base + 32] = edge[ROWS - HALO : ROWS - HALO + 16].astype(BF16)
-        north_ref[base : base + 16] = edge[0:16].astype(BF16)
-        north_ref[base + 16 : base + 32] = jnp.zeros((16, 2 * LANES), BF16)
+    for q in range(SLABS):
+        south_ref[EDGE * q : EDGE * (q + 1)] = own_ref[q, OWN - EDGE : OWN]
+        north_ref[EDGE * q : EDGE * (q + 1)] = own_ref[q, 0:EDGE]
+    base = EDGE * SLABS
+    south_ref[base : base + 16] = below_ref[...]
+    south_ref[base + 16 : base + 32] = edge[ROWS - HALO : ROWS - HALO + 16].astype(BF16)
+    north_ref[base : base + 16] = edge[0:16].astype(BF16)
+    north_ref[base + 16 : base + 32] = jnp.zeros((16, 2 * LANES), BF16)
 
     even = lax.rem(lat, 2) == 0
 
     @pl.when(even)
     def _():
-        write(pa_ref, pb_ref)
+        pa_ref[...] = south_ref[...]
 
     @pl.when(jnp.logical_not(even))
     def _():
-        write(pb_ref, pa_ref)
+        pa_ref[...] = north_ref[...]
 
 
 def band_kernel(
-    own_ref, below_ref, edge_ref, rb_ref, ra_ref,
+    own_ref, below_ref, edge_ref, down_ref, ra_ref, up_ref,
     band_ref, col_ref, pa_ref, pb_ref,
     north, south, tile, col,
 ):
@@ -137,12 +137,12 @@
     @pl.when(even_lat)
     def _():
         south[...] = ra_ref[...]
-        north[...] = rb_ref[...]
+        north[...] = down_ref[...]
 
     @pl.when(jnp.logical_not(even_lat))
     def _():
         north[...] = ra_ref[...]
-        south[...] = rb_ref[...]
+        south[...] = up_ref[...]
 
     base = EDGE * SLABS
     col[HALO : HALO + ROWS + 16] = edge_ref[...].astype(F32)
@@ -192,7 +192,7 @@
 
 
 def half_sums(
-    side_west, band_ref, col_ref, far_ref, w1_ref, b1_ref, w2_ref, load, sums,
+    side_west, band_ref, col_ref, from_west, from_east, w1_ref, b1_ref, w2_ref, load, sums,
     west_col, joined, ext, hidden,
 ):
     lat = lax.axis_index("lat")
@@ -204,9 +204,9 @@
 
     @pl.when(side_west)
     def _():
-        west_col[...] = far_ref[EXT * HALO_SLABS :].astype(F32)
+        west_col[...] = from_west[EXT * HALO_SLABS :].astype(F32)
         for k in range(HALO_SLABS):
-            ext[k] = far_ref[EXT * k : EXT * (k + 1)]
+            ext[k] = from_west[EXT * k : EXT * (k + 1)]
         for k in range(1, HALO_SLABS):
             ext[HALO_SLABS + k] = band_ref[k]
         for h, at in enumerate(halves):
@@ -216,11 +216,11 @@
     def _():
         west_col[...] = col_ref[...].astype(F32)
         for k in range(1, HALO_SLABS):
-            ext[HALO_SLABS + k] = far_ref[EXT * k : EXT * (k + 1)]
+            ext[HALO_SLABS + k] = from_east[EXT * k : EXT * (k + 1)]
         for k in range(HALO_SLABS):
             ext[k] = band_ref[k + 1]
         for h, at in enumerate(halves):
-            joined[h] = far_ref[0:EXT, at].astype(F32)
+            joined[h] = from_east[0:EXT, at].astype(F32)
 
     for h, at in enumerate(halves):
         joined[h, firsts, :] += west_col[0:EXT_R, at]
@@ -262,7 +262,7 @@
 
 
 def near_kernel(
-    band_ref, col_ref, far_ref, w1_ref, b1_ref, w2_hbm, b2_ref,
+    band_ref, col_ref, both_ref, w1_ref, b1_ref, w2_hbm, b2_ref,
     sums_ref,
     w2_ref, w2_sem, west_col, joined, ext, hidden,
 ):
@@ -271,7 +271,7 @@
     sums_ref[...] = jnp.broadcast_to(b2_ref[...], sums_ref.shape)
     odd = lax.rem(lax.axis_index("lon"), 2) == 1
     half_sums(
-        odd, band_ref, col_ref, far_ref, w1_ref, b1_ref, w2_ref, load, sums_ref,
+        odd, band_ref, col_ref, both_ref.at[0], both_ref.at[1], w1_ref, b1_ref, w2_ref, load, sums_ref,
         west_col, joined, ext, hidden,
     )
 
@@ -287,7 +287,7 @@
     sums[...] = near_ref[...]
     even = lax.rem(lax.axis_index("lon"), 2) == 0
     half_sums(
-        even, band_ref, col_ref, far_ref, w1_ref, b1_ref, w2_ref, load, sums,
+        even, band_ref, col_ref, far_ref, far_ref, w1_ref, b1_ref, w2_ref, load, sums,
         west_col, joined, ext, hidden,
     )
     for k in range(SLABS):
@@ -323,7 +323,7 @@
 
     lat_rows = SLABS * EDGE + 32
     lon_rows = HALO_SLABS * EXT + 64
-    own, below, edge, keep, lat_a, lat_b = pl.pallas_call(
+    own, below, edge, keep, to_south, to_partner, to_north = pl.pallas_call(
         down_kernel,
         out_shape=(
             shape(SLABS, OWN, chans),
@@ -332,9 +332,10 @@
             shape(SLABS, OWN, LANES, dtype=F32),
             shape(lat_rows, chans),
             shape(lat_rows, chans),
+            shape(lat_rows, chans),
         ),
         in_specs=[hbm] * 4,
-        out_specs=[vmem] * 6,
+        out_specs=[vmem] * 7,
         scratch_shapes=[
             pltpu.VMEM((2, 2 * ROWS, 2 * COLS, LANES), F32),
             pltpu.VMEM((COLS, ROWS), jnp.int32),
@@ -350,8 +351,13 @@
         name="down",
     )(in_hbm(fields), in_hbm(land_sea.T), in_hbm(w_depth), in_hbm(b_depth[None]))
 
-    got_b = lax.ppermute(lat_b, "lat", partners("lat", 1, False))
-    got_a = lax.ppermute(lat_a, "lat", partners("lat", 0, False))
+    swaps = partners("lat", 1, False)
+    got_down = lax.ppermute(to_south, "lat", [(i, j) for i, j in swaps if i < j])
+    got_a = lax.ppermute(to_partner, "lat", partners("lat", 0, False))
+    got_up = lax.ppermute(to_north, "lat", [(i, j) for i, j in swaps if i > j])
+
+    w_one = with_layout_constraint(w_one, Layout((0, 1, 2, 3)))
+    got_down, w_one = lax.optimization_barrier((got_down, w_one))
 
     band, col, lon_a, lon_b = pl.pallas_call(
         band_kernel,
@@ -361,7 +367,7 @@
             shape(lon_rows, chans),
             shape(lon_rows, chans),
         ),
-        in_specs=[vmem] * 5,
+        in_specs=[vmem] * 6,
         out_specs=[vmem] * 4,
         scratch_shapes=[
             pltpu.VMEM((lat_rows, chans), BF16),
@@ -371,10 +377,12 @@
         ],
         compiler_params=pltpu.CompilerParams(vmem_limit_bytes=10 << 20),
         name="band",
-    )(own, below, edge, got_b, got_a)
+    )(own, below, edge, got_down, got_a, got_up)
 
     got_b = lax.ppermute(lon_b, "lon", partners("lon", 1, True))
-    got_a = lax.ppermute(lon_a, "lon", partners("lon", 0, True))
+    count = lax.axis_size("lon")
+    chips = [[i, i + 1] for i in range(0, count, 2)]
+    both = lax.all_gather(lon_a, "lon", axis_index_groups=chips)
 
     scratch = [
         pltpu.VMEM(w_two.shape, BF16),
@@ -396,7 +404,7 @@
         compiler_params=pltpu.CompilerParams(vmem_limit_bytes=14 << 20),
         cost_estimate=cost,
         name="near_half",
-    )(band, col, got_a, w_one, b_one, w_two, b_two[None])
+    )(band, col, both, w_one, b_one, w_two, b_two[None])
 
     return pl.pallas_call(
         far_kernel,

time: 43.9 us -> 41.7 us (0.950)
  waiting for transfers between devices: 8 us -> 4.89 us
  blocking collectives: 0 us -> 2.8 us
  starting transfers between devices: 21.5 us -> 20.3 us
  Pallas kernels: 11.4 us -> 10.4 us
    ppermute x3, waiting for transfers between devices: 3.61 us -> 0.01 us  [the longest x1 0.01 us: on_device(): got_up = lax.ppermute(to_north, 'lat', [(i, j) for i, j in swaps if i > j])]
    all_gather x0 -> x1, blocking collectives: none -> 2.8 us  [on_device(): both = lax.all_gather(lon_a, 'lon', axis_index_groups=chips)]
    ppermute x3, starting transfers between devices: 18.8 us -> 16.4 us  [the longest x1 8.38 us: on_device(): got_up = lax.ppermute(to_north, 'lat', [(i, j) for i, j in swaps if i > j])]
    ppermute x1, starting transfers between devices: 2.67 us -> 3.9 us  [on_device(): got_b = lax.ppermute(lon_b, 'lon', partners('lon', 1, True))]
    pallas_call x1, Pallas kernels: 1 us -> 0.15 us  [on_device(): pl.pallas_call(band_kernel, out_shape=(shape(SLABS, EXT, chans), shape(64...]
    ppermute x1, waiting for transfers between devices: 4.39 us -> 4.88 us  [on_device(): got_b = lax.ppermute(lon_b, 'lon', partners('lon', 1, True))]
  transfers between devices with their start and end apart: 4 -> 4, of which waited for: 3 -> 1; matrix products, arithmetic and copies ran while one was open for 6% -> 7% of each run, Pallas kernels for 8% -> 8%
where the time goes in v4:
time: 41.7 us; the launch traced here: 41.2 us
  starting transfers between devices  20.3 us (49%)
  Pallas kernels  10.4 us (25%)
  waiting for transfers between devices  4.89 us (12%)
  blocking collectives  2.8 us (7%)
  local copies, waits for them, and re-layouts  2.7 us (6%)
    ppermute x1, starting transfers between devices, on_device(): got_up = lax.ppermute(to_north, 'lat', [(i, j) for i, j in swaps if i > j])  8.38 us
    ppermute x1, starting transfers between devices, on_device(): got_a = lax.ppermute(to_partner, 'lat', partners('lat', 0, False))  6.71 us
    ppermute x1, waiting for transfers between devices, on_device(): got_b = lax.ppermute(lon_b, 'lon', partners('lon', 1, True))  4.88 us
    pallas_call x1, Pallas kernels, on_device(): pl.pallas_call(far_kernel, out_shape=shape(ROWS, COLS, out_ch, dtype=F32)...  4.63 us
    ppermute x1, starting transfers between devices, on_device(): got_b = lax.ppermute(lon_b, 'lon', partners('lon', 1, True))  3.9 us
    pallas_call x1, Pallas kernels, on_device(): pl.pallas_call(near_kernel, out_shape=shape(SLABS, OWN, out_ch, dtype=F32...  3.48 us
    all_gather x1, blocking collectives, on_device(): both = lax.all_gather(lon_a, 'lon', axis_index_groups=chips)  2.8 us
    unnamed x5, local copies, waits for them, and re-layouts  2.69 us
  transfers between devices with their start and end apart: 4, of which 1 were waited for; matrix products, arithmetic and copies ran while one was open for 7% of the time, Pallas kernels for 8%

profile of v4, /device:TPU:57, one launch (start us, length us, event | category | flops | bytes accessed | tf_op | source)
XLA Modules:
  0.0 41.2 jit_solution(448600427319147469)
XLA Ops:
  0.0 2.2 %down.1 = (bf16[4,128,256]{2,1,0:T(8,128)(2,1)S(1)}, bf16[16,256]{1,0:T(8,128)(2,1)S(1)}, bf16[48,256]{1,0:T(8,128)(2,1)S(1)}, f32[4,128,128]{2,1,0:T(8,128)S(1)...) custom-call(f32[64,32,256]{2,1,0:T(8,128)} %f_hbm.1, ...), custom_call_target="tpu_custom_call" | custom-call | tf_op jit(solution)/shard_map/down/pallas_call | solution.py:326
  2.2 0.0 copy-start
  2.2 0.0 copy-start.1
  2.2 1.3 %collective-permute-start = (bf16[224,256]{1,0:T(8,128)(2,1)S(1)}, bf16[224,256]{1,0:T(8,128)(2,1)S(1)}, u32[]{:S(2)}, u32[]{:S(2)}) collective-permute-start(bf16[224,256]{1,0:T(8,128)(2,1)S(1)} %get-tuple-element.21), channel_id=1, source_target_pairs={{32,64},{96,128},{160,192},{224,256},{288,320},{352,384},{416,448}... | collective-permute-start | bytes 344072 | tf_op jit(solution)/shard_map/ppermute | solution.py:355
  3.5 6.7 %collective-permute-start.1 = (bf16[224,256]{1,0:T(8,128)(2,1)S(1)}, bf16[224,256]{1,0:T(8,128)(2,1)S(1)}, u32[]{:S(2)}, u32[]{:S(2)}) collective-permute-start(bf16[224,256]{1,0:T(8,128)(2,1)S(1)} %get-tuple-element.23), channel_id=1, source_target_pairs={{0,32},{32,0},{64,96},{96,64},{128,160},{160,128},{192,224},{224,1... | collective-permute-start | bytes 344072 | tf_op jit(solution)/shard_map/ppermute | solution.py:356
  10.2 8.4 %collective-permute-start.2 = (bf16[224,256]{1,0:T(8,128)(2,1)S(1)}, bf16[224,256]{1,0:T(8,128)(2,1)S(1)}, u32[]{:S(2)}, u32[]{:S(2)}) collective-permute-start(bf16[224,256]{1,0:T(8,128)(2,1)S(1)} %get-tuple-element.24), channel_id=1, source_target_pairs={{64,32},{128,96},{192,160},{256,224},{320,288},{384,352},{448,416}... | collective-permute-start | bytes 344072 | tf_op jit(solution)/shard_map/ppermute | solution.py:357
  18.6 2.7 %copy.9.w1_ref = bf16[3,3,256,300]{3,2,1,0:T(8,128)(2,1)S(1)} copy(bf16[3,3,256,300]{2,3,1,0:T(8,128)(2,1)} %param.12) | data formatting | bytes 2764800 | tf_op args[4]
  21.3 0.0 collective-permute-done.down_ref
  21.3 0.0 collective-permute-done.1.ra_ref
  21.3 0.0 collective-permute-done.2.up_ref
  21.3 0.1 band.1
  21.5 3.9 %collective-permute-start.3 = (bf16[736,256]{1,0:T(8,128)(2,1)S(1)}, bf16[736,256]{1,0:T(8,128)(2,1)S(1)}, u32[]{:S(2)}, u32[]{:S(2)}) collective-permute-start(bf16[736,256]{1,0:T(8,128)(2,1)S(1)} %get-tuple-element.27), channel_id=1, source_target_pairs={{1,2},{2,1},{3,4},{4,3},{5,6},{6,5},{7,8},{8,7},{9,10},{10,9},{11,... | collective-permute-start | bytes 1130504 | tf_op jit(solution)/shard_map/ppermute | solution.py:382
  25.4 0.0 copy-done
  25.4 0.0 copy-done.1
  25.4 2.8 %all-gather = bf16[1472,256]{1,0:T(8,128)(2,1)S(1)} all-gather(bf16[736,256]{1,0:T(8,128)(2,1)S(1)} %get-tuple-element.29), channel_id=2, replica_groups={{0,1},{2,3},{4,5},{6,7},{8,9},{10,11},{12,13},{14,15},{16,17},{18,19},{..., dimensions={0}, use_global_device_ids=true | all-gather | bytes 1130496 | tf_op jit(solution)/shard_map/all_gather | solution.py:385
  28.2 3.5 %near_half.1.near_ref = f32[4,128,300]{2,1,0:T(8,128)S(1)} custom-call(bf16[4,224,256]{2,1,0:T(8,128)(2,1)S(1)} %get-tuple-element.25.band_ref, bf16[64,256]{1,0:T(8,128)(2,1)S(1)} %get-tuple-element.26.col_ref, bf16[2,736,256]{2,1,0:T(8,128)(2,1)S(1)} %bitcast.3, bf16[3,3,256,300]{3,2,1,0:T(8,128)(2,1)S(1)} %copy.9.w1_ref, ...), custom_call_target="tpu_custom_call" | custom-call | flops 1476403200 | bytes 4194304 | tf_op jit(solution)/shard_map/near_half/pallas_call | solution.py:398
  31.7 4.9 %collective-permute-done.3.far_ref = bf16[736,256]{1,0:T(8,128)(2,1)S(1)} collective-permute-done((bf16[736,256]{1,0:T(8,128)(2,1)S(1)}, bf16[736,256]{1,0:T(8,128)(2,1)S(1)}, u32[]{:S(2)}, u32[]{:S(2)}) %collective-permute-start.3) | collective-permute-done | bytes 376864 | tf_op jit(solution)/shard_map/ppermute | solution.py:382
  36.6 4.6 %far_half.1 = f32[32,16,300]{2,1,0:T(8,128)} custom-call(bf16[4,224,256]{2,1,0:T(8,128)(2,1)S(1)} %get-tuple-element.25.band_ref, bf16[64,256]{1,0:T(8,128)(2,1)S(1)} %get-tuple-element.26.col_ref, bf16[736,256]{1,0:T(8,128)(2,1)S(1)} %collective-permute-done.3.far_ref, bf16[3,3,256,300]{3,2,1,0:T(8,128)(2,1)S(1)} %copy.9.w1_ref, ...), custom_call_target="tpu_custom_call" | custom-call | flops 1476403200 | bytes 4194304 | tf_op jit(solution)/shard_map/far_half/pallas_call | solution.py:409
  (2 shorter events, 0.0 us)
Async XLA Ops:
  2.2 23.2 %copy-start = (f32[300]{0:T(512)S(1)}, f32[300]{0:T(512)}, u32[]{:S(2)}) copy-start(f32[300]{0:T(512)} %param.13) | copy-start | bytes 3604
  2.2 23.2 %copy-start.1 = (f32[300]{0:T(512)S(1)}, f32[300]{0:T(512)}, u32[]{:S(2)}) copy-start(f32[300]{0:T(512)} %param.15) | copy-start | bytes 3604
  2.2 19.1 %collective-permute-start = (bf16[224,256]{1,0:T(8,128)(2,1)S(1)}, bf16[224,256]{1,0:T(8,128)(2,1)S(1)}, u32[]{:S(2)}, u32[]{:S(2)}) collective-permute-start(bf16[224,256]{1,0:T(8,128)(2,1)S(1)} %get-tuple-element.21), channel_id=1, source_target_pairs={{32,64},{96,128},{160,192},{224,256},{288,320},{352,384},{416,448}... | collective-permute-start | bytes 344072 | tf_op jit(solution)/shard_map/ppermute | solution.py:355
  3.5 17.8 %collective-permute-start.1 = (bf16[224,256]{1,0:T(8,128)(2,1)S(1)}, bf16[224,256]{1,0:T(8,128)(2,1)S(1)}, u32[]{:S(2)}, u32[]{:S(2)}) collective-permute-start(bf16[224,256]{1,0:T(8,128)(2,1)S(1)} %get-tuple-element.23), channel_id=1, source_target_pairs={{0,32},{32,0},{64,96},{96,64},{128,160},{160,128},{192,224},{224,1... | collective-permute-start | bytes 344072 | tf_op jit(solution)/shard_map/ppermute | solution.py:356
  10.2 11.1 %collective-permute-start.2 = (bf16[224,256]{1,0:T(8,128)(2,1)S(1)}, bf16[224,256]{1,0:T(8,128)(2,1)S(1)}, u32[]{:S(2)}, u32[]{:S(2)}) collective-permute-start(bf16[224,256]{1,0:T(8,128)(2,1)S(1)} %get-tuple-element.24), channel_id=1, source_target_pairs={{64,32},{128,96},{192,160},{256,224},{320,288},{384,352},{448,416}... | collective-permute-start | bytes 344072 | tf_op jit(solution)/shard_map/ppermute | solution.py:357
  21.5 15.1 %collective-permute-start.3 = (bf16[736,256]{1,0:T(8,128)(2,1)S(1)}, bf16[736,256]{1,0:T(8,128)(2,1)S(1)}, u32[]{:S(2)}, u32[]{:S(2)}) collective-permute-start(bf16[736,256]{1,0:T(8,128)(2,1)S(1)} %get-tuple-element.27), channel_id=1, source_target_pairs={{1,2},{2,1},{3,4},{4,3},{5,6},{6,5},{7,8},{8,7},{9,10},{10,9},{11,... | collective-permute-start | bytes 1130504 | tf_op jit(solution)/shard_map/ppermute | solution.py:382

commit v5 on v4

--- a/solution.py
+++ b/solution.py
@@ -19,6 +19,8 @@
 SIDE = (COLS + 16) // GROUP // 2
 EDGE = HALO * GROUP
 LANES = 128
+MAIN = 256
+PAD = 64
 CHUNKS = 4
 MASKED = 2.0**100
 LIMIT = 2.0**90
@@ -129,7 +131,7 @@
 def band_kernel(
     own_ref, below_ref, edge_ref, down_ref, ra_ref, up_ref,
     band_ref, col_ref, pa_ref, pb_ref,
-    north, south, tile, col,
+    north, south, tile, col, far,
 ):
     even_lat = lax.rem(lax.axis_index("lat"), 2) == 0
     even_lon = lax.rem(lax.axis_index("lon"), 2) == 0
@@ -180,11 +182,13 @@
 
     @pl.when(even_lon)
     def _():
-        write(pa_ref, pb_ref)
+        write(pa_ref, far)
 
     @pl.when(jnp.logical_not(even_lon))
     def _():
-        write(pb_ref, pa_ref)
+        write(far, pa_ref)
+
+    pb_ref[...] = far[...]
 
 
 def gelu(x):
@@ -192,8 +196,8 @@
 
 
 def half_sums(
-    side_west, band_ref, col_ref, from_west, from_east, w1_ref, b1_ref, w2_ref, load, sums,
-    west_col, joined, ext, hidden,
+    side_west, band_ref, col_ref, from_west, from_east, w1_ref, b1_ref, w2_ref, load, sums, emit,
+    west_col, joined, ext, hidden, hidden_rest, w1_rest, w2_rest,
 ):
     lat = lax.axis_index("lat")
     last = lax.axis_size("lat") - 1
@@ -231,14 +235,39 @@
         jnp.logical_or(place >= 8 * GROUP, lat > 0),
         jnp.logical_or(place < HID - 8 * GROUP, lat < last),
     )
+    rest = out_ch - MAIN
+    w1_rest[...] = jnp.zeros_like(w1_rest)
+    for a in range(3):
+        for b in range(3):
+            w1_rest[b, :, PAD * a : PAD * a + rest] = w1_ref[a, b, :, MAIN:]
+    bias = b1_ref[:, :MAIN]
+    bias_rest = jnp.concatenate([b1_ref[:, MAIN:], jnp.zeros((1, PAD - rest), F32)], axis=1)
+    shift, reach = 4 * GROUP, 8 * GROUP
     for k in range(SIDE):
-        total = jnp.zeros((HID, out_ch), F32) + b1_ref[...]
+        total = jnp.zeros((HID, MAIN), F32) + bias
+        tail = jnp.zeros((EXT, 3 * PAD), F32)
+        for b in range(3):
+            for a in range(3):
+                piece = ext[k + b, shift * a : shift * a + HID]
+                total = total + jnp.dot(
+                    piece, w1_ref[a, b, :, :MAIN], preferred_element_type=F32
+                )
+            tail = tail + jnp.dot(ext[k + b], w1_rest[b], preferred_element_type=F32)
+        total_rest = bias_rest
         for a in range(3):
-            for b in range(3):
-                piece = ext[k + b, 4 * GROUP * a : 4 * GROUP * a + HID]
-                total = total + jnp.dot(piece, w1_ref[a, b], preferred_element_type=F32)
+            total_rest = total_rest + tail[shift * a : shift * a + HID, PAD * a : PAD * (a + 1)]
         hidden[k] = jnp.where(inside, gelu(total), 0.0).astype(BF16)
+        value = jnp.where(inside, gelu(total_rest), 0.0)
+        for a in range(3):
+            hidden_rest[k, :, PAD * a : PAD * (a + 1)] = value[
+                reach * a : reach * a + OWN
+            ].astype(BF16)
+
     load.wait()
+    w2_rest[...] = jnp.zeros_like(w2_rest)
+    for a in range(3):
+        for b in range(3):
+            w2_rest[b, PAD * a : PAD * a + rest] = w2_ref[a, b, MAIN:]
 
     def second(first_slab):
         for k in range(SLABS):
@@ -248,9 +277,14 @@
                 if slab < 0 or slab >= SIDE:
                     continue
                 for a in range(3):
-                    piece = hidden[slab, 8 * GROUP * a : 8 * GROUP * a + OWN]
-                    total = total + jnp.dot(piece, w2_ref[a, b], preferred_element_type=F32)
-            sums[k] = total
+                    piece = hidden[slab, reach * a : reach * a + OWN]
+                    total = total + jnp.dot(
+                        piece, w2_ref[a, b, :MAIN], preferred_element_type=F32
+                    )
+                total = total + jnp.dot(
+                    hidden_rest[slab], w2_rest[b], preferred_element_type=F32
+                )
+            emit(k, total)
 
     @pl.when(side_west)
     def _():
@@ -264,37 +298,42 @@
 def near_kernel(
     band_ref, col_ref, both_ref, w1_ref, b1_ref, w2_hbm, b2_ref,
     sums_ref,
-    w2_ref, w2_sem, west_col, joined, ext, hidden,
+    w2_ref, w2_sem, west_col, joined, ext, hidden, hidden_rest, w1_rest, w2_rest,
 ):
     load = pltpu.make_async_copy(w2_hbm, w2_ref, w2_sem)
     load.start()
-    sums_ref[...] = jnp.broadcast_to(b2_ref[...], sums_ref.shape)
+    start = jnp.broadcast_to(b2_ref[...], sums_ref.shape[1:])
+
+    def emit(k, total):
+        sums_ref[k] = total
+
     odd = lax.rem(lax.axis_index("lon"), 2) == 1
     half_sums(
-        odd, band_ref, col_ref, both_ref.at[0], both_ref.at[1], w1_ref, b1_ref, w2_ref, load, sums_ref,
-        west_col, joined, ext, hidden,
+        odd, band_ref, col_ref, both_ref.at[0], both_ref.at[1], w1_ref, b1_ref, w2_ref, load, [start] * SLABS, emit,
+        west_col, joined, ext, hidden, hidden_rest, w1_rest, w2_rest,
     )
 
 
 def far_kernel(
     band_ref, col_ref, far_ref, w1_ref, b1_ref, w2_hbm, near_ref, keep_ref,
     out_ref,
-    w2_ref, w2_sem, west_col, joined, ext, hidden, sums,
+    w2_ref, w2_sem, west_col, joined, ext, hidden, hidden_rest, w1_rest, w2_rest,
 ):
     load = pltpu.make_async_copy(w2_hbm, w2_ref, w2_sem)
     load.start()
     out_ch = b1_ref.shape[1]
-    sums[...] = near_ref[...]
+
+    def emit(k, total):
+        kept = keep_ref[k]
+        kept = jnp.concatenate([kept] * pl.cdiv(out_ch, LANES), axis=1)[:, :out_ch]
+        value = (gelu(total) * kept).reshape(ROWS, GROUP, out_ch)
+        out_ref[:, GROUP * k : GROUP * (k + 1), :] = value
+
     even = lax.rem(lax.axis_index("lon"), 2) == 0
     half_sums(
-        even, band_ref, col_ref, far_ref, far_ref, w1_ref, b1_ref, w2_ref, load, sums,
-        west_col, joined, ext, hidden,
+        even, band_ref, col_ref, far_ref, far_ref, w1_ref, b1_ref, w2_ref, load, near_ref, emit,
+        west_col, joined, ext, hidden, hidden_rest, w1_rest, w2_rest,
     )
-    for k in range(SLABS):
-        kept = keep_ref[k]
-        kept = jnp.concatenate([kept] * pl.cdiv(out_ch, LANES), axis=1)[:, :out_ch]
-        value = (gelu(sums[k]) * kept).reshape(ROWS, GROUP, out_ch)
-        out_ref[:, GROUP * k : GROUP * (k + 1), :] = value
 
 
 def partners(axis, start, periodic):
@@ -374,6 +413,7 @@
             pltpu.VMEM((lat_rows, chans), BF16),
             pltpu.VMEM((2, SLABS, 16, chans), F32),
             pltpu.VMEM((64, chans), F32),
+            pltpu.VMEM((lon_rows, chans), BF16),
         ],
         compiler_params=pltpu.CompilerParams(vmem_limit_bytes=10 << 20),
         name="band",
@@ -390,7 +430,10 @@
         pltpu.VMEM((64, chans), F32),
         pltpu.VMEM((2, EXT, LANES), F32),
         pltpu.VMEM((2 * HALO_SLABS, EXT, chans), BF16),
-        pltpu.VMEM((SIDE, HID, out_ch), BF16),
+        pltpu.VMEM((SIDE, HID, MAIN), BF16),
+        pltpu.VMEM((SIDE, OWN, 3 * PAD), BF16),
+        pltpu.VMEM((3, chans, 3 * PAD), BF16),
+        pltpu.VMEM((3, 3 * PAD, out_ch), BF16),
     ]
     w_two, b_one = in_hbm(w_two), b_one[None]
     flops = 2 * SIDE * HID * 9 * chans * out_ch + 2 * 6 * OWN * 3 * out_ch * out_ch
@@ -411,7 +454,7 @@
         out_shape=shape(ROWS, COLS, out_ch, dtype=F32),
         in_specs=[vmem] * 5 + [hbm, vmem, vmem],
         out_specs=vmem,
-        scratch_shapes=scratch + [pltpu.VMEM((SLABS, OWN, out_ch), F32)],
+        scratch_shapes=scratch,
         compiler_params=pltpu.CompilerParams(vmem_limit_bytes=14 << 20),
         cost_estimate=cost,
         name="far_half",

time: 41.7 us -> 40.8 us (0.978)
  Pallas kernels: 10.4 us -> 8.68 us
  waiting for transfers between devices: 4.89 us -> 5.68 us
    pallas_call x1, Pallas kernels: 4.63 us -> 3.64 us  [on_device(): pl.pallas_call(far_kernel, out_shape=shape(ROWS, COLS, out_ch, dtype=F32)...]
    ppermute x1, waiting for transfers between devices: 4.88 us -> 5.67 us  [on_device(): got_b = lax.ppermute(lon_b, 'lon', partners('lon', 1, True))]
    pallas_call x1, Pallas kernels: 3.48 us -> 2.69 us  [on_device(): pl.pallas_call(near_kernel, out_shape=shape(SLABS, OWN, out_ch, dtype=F32...]
  transfers between devices with their start and end apart: 4 -> 4, of which waited for: 1 -> 1; matrix products, arithmetic and copies ran while one was open for 7% -> 7% of each run, Pallas kernels for 8% -> 7%
where the time goes in v5:
time: 40.8 us; the launch traced here: 40.3 us
  starting transfers between devices  20.3 us (50%)
  Pallas kernels  8.68 us (21%)
  waiting for transfers between devices  5.68 us (14%)
  blocking collectives  2.8 us (7%)
  local copies, waits for them, and re-layouts  2.7 us (7%)
    ppermute x1, starting transfers between devices, on_device(): got_up = lax.ppermute(to_north, 'lat', [(i, j) for i, j in swaps if i > j])  8.38 us
    ppermute x1, starting transfers between devices, on_device(): got_a = lax.ppermute(to_partner, 'lat', partners('lat', 0, False))  6.71 us
    ppermute x1, waiting for transfers between devices, on_device(): got_b = lax.ppermute(lon_b, 'lon', partners('lon', 1, True))  5.67 us
    ppermute x1, starting transfers between devices, on_device(): got_b = lax.ppermute(lon_b, 'lon', partners('lon', 1, True))  3.9 us
    pallas_call x1, Pallas kernels, on_device(): pl.pallas_call(far_kernel, out_shape=shape(ROWS, COLS, out_ch, dtype=F32)...  3.64 us
    all_gather x1, blocking collectives, on_device(): both = lax.all_gather(lon_a, 'lon', axis_index_groups=chips)  2.8 us
    pallas_call x1, Pallas kernels, on_device(): pl.pallas_call(near_kernel, out_shape=shape(SLABS, OWN, out_ch, dtype=F32...  2.69 us
    unnamed x5, local copies, waits for them, and re-layouts  2.69 us
  transfers between devices with their start and end apart: 4, of which 1 were waited for; matrix products, arithmetic and copies ran while one was open for 7% of the time, Pallas kernels for 7%

profile of v5, /device:TPU:57, one launch (start us, length us, event | category | flops | bytes accessed | tf_op | source)
XLA Modules:
  0.0 40.3 jit_solution(6679538207281530677)
XLA Ops:
  0.0 2.2 %down.1 = (bf16[4,128,256]{2,1,0:T(8,128)(2,1)S(1)}, bf16[16,256]{1,0:T(8,128)(2,1)S(1)}, bf16[48,256]{1,0:T(8,128)(2,1)S(1)}, f32[4,128,128]{2,1,0:T(8,128)S(1)...) custom-call(f32[64,32,256]{2,1,0:T(8,128)} %f_hbm.1, ...), custom_call_target="tpu_custom_call" | custom-call | tf_op jit(solution)/shard_map/down/pallas_call | solution.py:365
  2.2 0.0 copy-start
  2.2 0.0 copy-start.1
  2.2 1.3 %collective-permute-start = (bf16[224,256]{1,0:T(8,128)(2,1)S(1)}, bf16[224,256]{1,0:T(8,128)(2,1)S(1)}, u32[]{:S(2)}, u32[]{:S(2)}) collective-permute-start(bf16[224,256]{1,0:T(8,128)(2,1)S(1)} %get-tuple-element.21), channel_id=1, source_target_pairs={{32,64},{96,128},{160,192},{224,256},{288,320},{352,384},{416,448}... | collective-permute-start | bytes 344072 | tf_op jit(solution)/shard_map/ppermute | solution.py:394
  3.5 6.7 %collective-permute-start.1 = (bf16[224,256]{1,0:T(8,128)(2,1)S(1)}, bf16[224,256]{1,0:T(8,128)(2,1)S(1)}, u32[]{:S(2)}, u32[]{:S(2)}) collective-permute-start(bf16[224,256]{1,0:T(8,128)(2,1)S(1)} %get-tuple-element.23), channel_id=1, source_target_pairs={{0,32},{32,0},{64,96},{96,64},{128,160},{160,128},{192,224},{224,1... | collective-permute-start | bytes 344072 | tf_op jit(solution)/shard_map/ppermute | solution.py:395
  10.2 8.4 %collective-permute-start.2 = (bf16[224,256]{1,0:T(8,128)(2,1)S(1)}, bf16[224,256]{1,0:T(8,128)(2,1)S(1)}, u32[]{:S(2)}, u32[]{:S(2)}) collective-permute-start(bf16[224,256]{1,0:T(8,128)(2,1)S(1)} %get-tuple-element.24), channel_id=1, source_target_pairs={{64,32},{128,96},{192,160},{256,224},{320,288},{384,352},{448,416}... | collective-permute-start | bytes 344072 | tf_op jit(solution)/shard_map/ppermute | solution.py:396
  18.6 2.7 %copy.9.w1_ref = bf16[3,3,256,300]{3,2,1,0:T(8,128)(2,1)S(1)} copy(bf16[3,3,256,300]{2,3,1,0:T(8,128)(2,1)} %param.12) | data formatting | bytes 2764800 | tf_op args[4]
  21.3 0.0 collective-permute-done.down_ref
  21.3 0.0 collective-permute-done.1.ra_ref
  21.3 0.0 collective-permute-done.2.up_ref
  21.3 0.2 band.1
  21.5 3.9 %collective-permute-start.3 = (bf16[736,256]{1,0:T(8,128)(2,1)S(1)}, bf16[736,256]{1,0:T(8,128)(2,1)S(1)}, u32[]{:S(2)}, u32[]{:S(2)}) collective-permute-start(bf16[736,256]{1,0:T(8,128)(2,1)S(1)} %get-tuple-element.27), channel_id=1, source_target_pairs={{1,2},{2,1},{3,4},{4,3},{5,6},{6,5},{7,8},{8,7},{9,10},{10,9},{11,... | collective-permute-start | bytes 1130504 | tf_op jit(solution)/shard_map/ppermute | solution.py:422
  25.4 0.0 copy-done
  25.4 0.0 copy-done.1
  25.5 2.8 %all-gather = bf16[1472,256]{1,0:T(8,128)(2,1)S(1)} all-gather(bf16[736,256]{1,0:T(8,128)(2,1)S(1)} %get-tuple-element.29), channel_id=2, replica_groups={{0,1},{2,3},{4,5},{6,7},{8,9},{10,11},{12,13},{14,15},{16,17},{18,19},{..., dimensions={0}, use_global_device_ids=true | all-gather | bytes 1130496 | tf_op jit(solution)/shard_map/all_gather | solution.py:425
  28.3 2.7 %near_half.1.near_ref = f32[4,128,300]{2,1,0:T(8,128)S(1)} custom-call(bf16[4,224,256]{2,1,0:T(8,128)(2,1)S(1)} %get-tuple-element.25.band_ref, bf16[64,256]{1,0:T(8,128)(2,1)S(1)} %get-tuple-element.26.col_ref, bf16[2,736,256]{2,1,0:T(8,128)(2,1)S(1)} %bitcast.3, bf16[3,3,256,300]{3,2,1,0:T(8,128)(2,1)S(1)} %copy.9.w1_ref, ...), custom_call_target="tpu_custom_call" | custom-call | flops 1476403200 | bytes 4194304 | tf_op jit(solution)/shard_map/near_half/pallas_call | solution.py:441
  31.0 5.7 %collective-permute-done.3.far_ref = bf16[736,256]{1,0:T(8,128)(2,1)S(1)} collective-permute-done((bf16[736,256]{1,0:T(8,128)(2,1)S(1)}, bf16[736,256]{1,0:T(8,128)(2,1)S(1)}, u32[]{:S(2)}, u32[]{:S(2)}) %collective-permute-start.3) | collective-permute-done | bytes 376864 | tf_op jit(solution)/shard_map/ppermute | solution.py:422
  36.6 3.6 %far_half.1 = f32[32,16,300]{2,1,0:T(8,128)} custom-call(bf16[4,224,256]{2,1,0:T(8,128)(2,1)S(1)} %get-tuple-element.25.band_ref, bf16[64,256]{1,0:T(8,128)(2,1)S(1)} %get-tuple-element.26.col_ref, bf16[736,256]{1,0:T(8,128)(2,1)S(1)} %collective-permute-done.3.far_ref, bf16[3,3,256,300]{3,2,1,0:T(8,128)(2,1)S(1)} %copy.9.w1_ref, ...), custom_call_target="tpu_custom_call" | custom-call | flops 1476403200 | bytes 4194304 | tf_op jit(solution)/shard_map/far_half/pallas_call | solution.py:452
  (2 shorter events, 0.0 us)
Async XLA Ops:
  2.2 23.2 %copy-start = (f32[300]{0:T(512)S(1)}, f32[300]{0:T(512)}, u32[]{:S(2)}) copy-start(f32[300]{0:T(512)} %param.13) | copy-start | bytes 3604
  2.2 23.2 %copy-start.1 = (f32[300]{0:T(512)S(1)}, f32[300]{0:T(512)}, u32[]{:S(2)}) copy-start(f32[300]{0:T(512)} %param.15) | copy-start | bytes 3604
  2.2 19.1 %collective-permute-start = (bf16[224,256]{1,0:T(8,128)(2,1)S(1)}, bf16[224,256]{1,0:T(8,128)(2,1)S(1)}, u32[]{:S(2)}, u32[]{:S(2)}) collective-permute-start(bf16[224,256]{1,0:T(8,128)(2,1)S(1)} %get-tuple-element.21), channel_id=1, source_target_pairs={{32,64},{96,128},{160,192},{224,256},{288,320},{352,384},{416,448}... | collective-permute-start | bytes 344072 | tf_op jit(solution)/shard_map/ppermute | solution.py:394
  3.5 17.8 %collective-permute-start.1 = (bf16[224,256]{1,0:T(8,128)(2,1)S(1)}, bf16[224,256]{1,0:T(8,128)(2,1)S(1)}, u32[]{:S(2)}, u32[]{:S(2)}) collective-permute-start(bf16[224,256]{1,0:T(8,128)(2,1)S(1)} %get-tuple-element.23), channel_id=1, source_target_pairs={{0,32},{32,0},{64,96},{96,64},{128,160},{160,128},{192,224},{224,1... | collective-permute-start | bytes 344072 | tf_op jit(solution)/shard_map/ppermute | solution.py:395
  10.2 11.1 %collective-permute-start.2 = (bf16[224,256]{1,0:T(8,128)(2,1)S(1)}, bf16[224,256]{1,0:T(8,128)(2,1)S(1)}, u32[]{:S(2)}, u32[]{:S(2)}) collective-permute-start(bf16[224,256]{1,0:T(8,128)(2,1)S(1)} %get-tuple-element.24), channel_id=1, source_target_pairs={{64,32},{128,96},{192,160},{256,224},{320,288},{384,352},{448,416}... | collective-permute-start | bytes 344072 | tf_op jit(solution)/shard_map/ppermute | solution.py:396
  21.5 15.1 %collective-permute-start.3 = (bf16[736,256]{1,0:T(8,128)(2,1)S(1)}, bf16[736,256]{1,0:T(8,128)(2,1)S(1)}, u32[]{:S(2)}, u32[]{:S(2)}) collective-permute-start(bf16[736,256]{1,0:T(8,128)(2,1)S(1)} %get-tuple-element.27), channel_id=1, source_target_pairs={{1,2},{2,1},{3,4},{4,3},{5,6},{6,5},{7,8},{8,7},{9,10},{10,9},{11,... | collective-permute-start | bytes 1130504 | tf_op jit(solution)/shard_map/ppermute | solution.py:422

commit v6 on v5

--- a/solution.py
+++ b/solution.py
@@ -2,7 +2,6 @@
 import jax.numpy as jnp
 from jax import lax
 from jax.experimental import pallas as pl
-from jax.experimental.layout import Layout, with_layout_constraint
 from jax.experimental.pallas import tpu as pltpu
 from jax.sharding import PartitionSpec as P
 
@@ -18,6 +17,8 @@
 HID = (ROWS + 16) * GROUP
 SIDE = (COLS + 16) // GROUP // 2
 EDGE = HALO * GROUP
+EARLY = OWN - 16
+LATE = EXT - EARLY
 LANES = 128
 MAIN = 256
 PAD = 64
@@ -128,10 +129,28 @@
         pa_ref[...] = north_ref[...]
 
 
+def early_kernel(own_ref, edge_ref, early_ref, edge):
+    even = lax.rem(lax.axis_index("lon"), 2) == 0
+    edge[...] = edge_ref[...].astype(F32)
+    base = EARLY * HALO_SLABS
+
+    @pl.when(even)
+    def _():
+        for k in range(HALO_SLABS):
+            early_ref[EARLY * k : EARLY * (k + 1)] = own_ref[k, 16:OWN]
+        early_ref[base:] = jnp.zeros_like(early_ref[base:])
+
+    @pl.when(jnp.logical_not(even))
+    def _():
+        for k in range(HALO_SLABS):
+            early_ref[EARLY * k : EARLY * (k + 1)] = own_ref[SLABS - HALO_SLABS + k, 16:OWN]
+        early_ref[base:] = edge[4:36].astype(BF16)
+
+
 def band_kernel(
     own_ref, below_ref, edge_ref, down_ref, ra_ref, up_ref,
     band_ref, col_ref, pa_ref, pb_ref,
-    north, south, tile, col, far,
+    north, south, tile, col,
 ):
     even_lat = lax.rem(lax.axis_index("lat"), 2) == 0
     even_lon = lax.rem(lax.axis_index("lon"), 2) == 0
@@ -174,21 +193,33 @@
         band_ref[q, EDGE + OWN + 16 : EXT] = south[EDGE * q + 16 : EDGE * (q + 1)]
 
     def write(east_ref, west_ref):
+        top, late = 64, LATE - 64
         for k in range(HALO_SLABS):
-            east_ref[EXT * k : EXT * (k + 1)] = band_ref[SLABS - HALO_SLABS + k]
-            west_ref[EXT * k : EXT * (k + 1)] = band_ref[k]
-        east_ref[EXT * HALO_SLABS :] = col_ref[...]
-        west_ref[EXT * HALO_SLABS :] = jnp.zeros_like(col_ref)
+            for ref, q, full in (
+                (east_ref, SLABS - HALO_SLABS + k, east_ref is pa_ref),
+                (west_ref, k, west_ref is pa_ref),
+            ):
+                if full:
+                    ref[EXT * k : EXT * (k + 1)] = band_ref[q]
+                else:
+                    ref[LATE * k : LATE * k + top] = band_ref[q, 0:top]
+                    ref[LATE * k + top : LATE * (k + 1)] = band_ref[q, EXT - late : EXT]
+        if east_ref is pa_ref:
+            east_ref[EXT * HALO_SLABS :] = col_ref[...]
+            west_ref[LATE * HALO_SLABS :] = jnp.zeros_like(west_ref[LATE * HALO_SLABS :])
+        else:
+            base = LATE * HALO_SLABS
+            east_ref[base : base + 16] = col[0:16].astype(BF16)
+            east_ref[base + 16 : base + 32] = col[EXT_R - HALO : EXT_R + 4].astype(BF16)
+            west_ref[EXT * HALO_SLABS :] = jnp.zeros_like(col_ref)
 
     @pl.when(even_lon)
     def _():
-        write(pa_ref, far)
+        write(pa_ref, pb_ref)
 
     @pl.when(jnp.logical_not(even_lon))
     def _():
-        write(far, pa_ref)
-
-    pb_ref[...] = far[...]
+        write(pb_ref, pa_ref)
 
 
 def gelu(x):
@@ -196,8 +227,8 @@
 
 
 def half_sums(
-    side_west, band_ref, col_ref, from_west, from_east, w1_ref, b1_ref, w2_ref, load, sums, emit,
-    west_col, joined, ext, hidden, hidden_rest, w1_rest, w2_rest,
+    side_west, band_ref, col_ref, from_west, from_east, w1_ref, w1_rest, b1_ref, w2_ref, load, sums, emit,
+    west_col, joined, ext, hidden, hidden_rest, w2_rest,
 ):
     lat = lax.axis_index("lat")
     last = lax.axis_size("lat") - 1
@@ -236,21 +267,17 @@
         jnp.logical_or(place < HID - 8 * GROUP, lat < last),
     )
     rest = out_ch - MAIN
-    w1_rest[...] = jnp.zeros_like(w1_rest)
-    for a in range(3):
-        for b in range(3):
-            w1_rest[b, :, PAD * a : PAD * a + rest] = w1_ref[a, b, :, MAIN:]
     bias = b1_ref[:, :MAIN]
     bias_rest = jnp.concatenate([b1_ref[:, MAIN:], jnp.zeros((1, PAD - rest), F32)], axis=1)
     shift, reach = 4 * GROUP, 8 * GROUP
     for k in range(SIDE):
         total = jnp.zeros((HID, MAIN), F32) + bias
-        tail = jnp.zeros((EXT, 3 * PAD), F32)
+        tail = jnp.zeros((EXT, MAIN), F32)
         for b in range(3):
             for a in range(3):
                 piece = ext[k + b, shift * a : shift * a + HID]
                 total = total + jnp.dot(
-                    piece, w1_ref[a, b, :, :MAIN], preferred_element_type=F32
+                    piece, w1_ref[a, b], preferred_element_type=F32
                 )
             tail = tail + jnp.dot(ext[k + b], w1_rest[b], preferred_element_type=F32)
         total_rest = bias_rest
@@ -296,12 +323,19 @@
 
 
 def near_kernel(
-    band_ref, col_ref, both_ref, w1_ref, b1_ref, w2_hbm, b2_ref,
-    sums_ref,
-    w2_ref, w2_sem, west_col, joined, ext, hidden, hidden_rest, w1_rest, w2_rest,
+    band_ref, col_ref, both_ref, stored_ref, b1_ref, w2_hbm, b2_ref,
+    sums_ref, w1_ref, w1_rest,
+    w2_ref, w2_sem, west_col, joined, ext, hidden, hidden_rest, w2_rest, stack,
 ):
     load = pltpu.make_async_copy(w2_hbm, w2_ref, w2_sem)
     load.start()
+    rest = stored_ref.shape[2] - MAIN
+    stack[...] = jnp.zeros_like(stack)
+    for b in range(3):
+        for a in range(3):
+            w1_ref[a, b] = stored_ref[a, b, :MAIN].T
+            stack[b, PAD * a : PAD * a + rest] = stored_ref[a, b, MAIN:]
+        w1_rest[b] = stack[b].T
     start = jnp.broadcast_to(b2_ref[...], sums_ref.shape[1:])
 
     def emit(k, total):
@@ -309,19 +343,30 @@
 
     odd = lax.rem(lax.axis_index("lon"), 2) == 1
     half_sums(
-        odd, band_ref, col_ref, both_ref.at[0], both_ref.at[1], w1_ref, b1_ref, w2_ref, load, [start] * SLABS, emit,
-        west_col, joined, ext, hidden, hidden_rest, w1_rest, w2_rest,
+        odd, band_ref, col_ref, both_ref.at[0], both_ref.at[1], w1_ref, w1_rest, b1_ref, w2_ref, load, [start] * SLABS, emit,
+        west_col, joined, ext, hidden, hidden_rest, w2_rest,
     )
 
 
 def far_kernel(
-    band_ref, col_ref, far_ref, w1_ref, b1_ref, w2_hbm, near_ref, keep_ref,
+    band_ref, col_ref, early_ref, late_ref, w1_ref, w1_rest, b1_ref, w2_hbm, near_ref, keep_ref,
     out_ref,
-    w2_ref, w2_sem, west_col, joined, ext, hidden, hidden_rest, w1_rest, w2_rest,
+    w2_ref, w2_sem, west_col, joined, ext, hidden, hidden_rest, w2_rest, far_ref, far_col,
 ):
     load = pltpu.make_async_copy(w2_hbm, w2_ref, w2_sem)
     load.start()
     out_ch = b1_ref.shape[1]
+    for k in range(HALO_SLABS):
+        at = EXT * k
+        far_ref[at : at + 64] = late_ref[LATE * k : LATE * k + 64]
+        far_ref[at + 64 : at + 64 + EARLY] = early_ref[EARLY * k : EARLY * (k + 1)]
+        far_ref[at + 64 + EARLY : at + EXT] = late_ref[LATE * k + 64 : LATE * (k + 1)]
+    base = LATE * HALO_SLABS
+    far_col[0:16] = late_ref[base : base + 16].astype(F32)
+    far_col[16:48] = early_ref[EARLY * HALO_SLABS :].astype(F32)
+    far_col[EXT_R - HALO : EXT_R + 4] = late_ref[base + 16 : base + 32].astype(F32)
+    far_col[EXT_R + 4 :] = jnp.zeros_like(far_col[EXT_R + 4 :])
+    far_ref[EXT * HALO_SLABS :] = far_col[...].astype(BF16)
 
     def emit(k, total):
         kept = keep_ref[k]
@@ -331,8 +376,8 @@
 
     even = lax.rem(lax.axis_index("lon"), 2) == 0
     half_sums(
-        even, band_ref, col_ref, far_ref, far_ref, w1_ref, b1_ref, w2_ref, load, near_ref, emit,
-        west_col, joined, ext, hidden, hidden_rest, w1_rest, w2_rest,
+        even, band_ref, col_ref, far_ref, far_ref, w1_ref, w1_rest, b1_ref, w2_ref, load, near_ref, emit,
+        west_col, joined, ext, hidden, hidden_rest, w2_rest,
     )
 
 
@@ -395,8 +440,17 @@
     got_a = lax.ppermute(to_partner, "lat", partners("lat", 0, False))
     got_up = lax.ppermute(to_north, "lat", [(i, j) for i, j in swaps if i > j])
 
-    w_one = with_layout_constraint(w_one, Layout((0, 1, 2, 3)))
-    got_down, w_one = lax.optimization_barrier((got_down, w_one))
+    early_rows = EARLY * HALO_SLABS + 32
+    early = pl.pallas_call(
+        early_kernel,
+        out_shape=shape(early_rows, chans),
+        in_specs=[vmem] * 2,
+        out_specs=vmem,
+        scratch_shapes=[pltpu.VMEM((ROWS + 16, chans), F32)],
+        compiler_params=pltpu.CompilerParams(vmem_limit_bytes=4 << 20),
+        name="early",
+    )(own, edge)
+    got_early = lax.ppermute(early, "lon", partners("lon", 1, True))
 
     band, col, lon_a, lon_b = pl.pallas_call(
         band_kernel,
@@ -404,7 +458,7 @@
             shape(SLABS, EXT, chans),
             shape(64, chans),
             shape(lon_rows, chans),
-            shape(lon_rows, chans),
+            shape(LATE * HALO_SLABS + 32, chans),
         ),
         in_specs=[vmem] * 6,
         out_specs=[vmem] * 4,
@@ -413,7 +467,6 @@
             pltpu.VMEM((lat_rows, chans), BF16),
             pltpu.VMEM((2, SLABS, 16, chans), F32),
             pltpu.VMEM((64, chans), F32),
-            pltpu.VMEM((lon_rows, chans), BF16),
         ],
         compiler_params=pltpu.CompilerParams(vmem_limit_bytes=10 << 20),
         name="band",
@@ -432,33 +485,37 @@
         pltpu.VMEM((2 * HALO_SLABS, EXT, chans), BF16),
         pltpu.VMEM((SIDE, HID, MAIN), BF16),
         pltpu.VMEM((SIDE, OWN, 3 * PAD), BF16),
-        pltpu.VMEM((3, chans, 3 * PAD), BF16),
         pltpu.VMEM((3, 3 * PAD, out_ch), BF16),
     ]
     w_two, b_one = in_hbm(w_two), b_one[None]
     flops = 2 * SIDE * HID * 9 * chans * out_ch + 2 * 6 * OWN * 3 * out_ch * out_ch
     cost = pl.CostEstimate(flops=flops, bytes_accessed=4 << 20, transcendentals=SIDE * HID * out_ch)
-    near = pl.pallas_call(
+    near, w1_main, w1_rest = pl.pallas_call(
         near_kernel,
-        out_shape=shape(SLABS, OWN, out_ch, dtype=F32),
+        out_shape=(
+            shape(SLABS, OWN, out_ch, dtype=F32),
+            shape(3, 3, chans, MAIN),
+            shape(3, chans, MAIN),
+        ),
         in_specs=[vmem] * 5 + [hbm, vmem],
-        out_specs=vmem,
-        scratch_shapes=scratch,
+        out_specs=[vmem] * 3,
+        scratch_shapes=scratch + [pltpu.VMEM((3, MAIN, chans), BF16)],
         compiler_params=pltpu.CompilerParams(vmem_limit_bytes=14 << 20),
         cost_estimate=cost,
         name="near_half",
-    )(band, col, both, w_one, b_one, w_two, b_two[None])
+    )(band, col, both, w_one.transpose(0, 1, 3, 2), b_one, w_two, b_two[None])
 
     return pl.pallas_call(
         far_kernel,
         out_shape=shape(ROWS, COLS, out_ch, dtype=F32),
-        in_specs=[vmem] * 5 + [hbm, vmem, vmem],
+        in_specs=[vmem] * 7 + [hbm, vmem, vmem],
         out_specs=vmem,
-        scratch_shapes=scratch,
+        scratch_shapes=scratch
+        + [pltpu.VMEM((lon_rows, chans), BF16), pltpu.VMEM((64, chans), F32)],
         compiler_params=pltpu.CompilerParams(vmem_limit_bytes=14 << 20),
         cost_estimate=cost,
         name="far_half",
-    )(band, col, got_b, w_one, b_one, w_two, near, keep)
+    )(band, col, got_early, got_b, w1_main, w1_rest, b_one, w_two, near, keep)
 
 
 def solution(mesh):

time: 40.8 us -> 38 us (0.931)
  waiting for transfers between devices: 5.68 us -> 1.05 us
  starting transfers between devices: 20.3 us -> 24.6 us
  local copies, waits for them, and re-layouts: 2.7 us -> 0.02 us
  Pallas kernels: 8.68 us -> 9.14 us
  blocking collectives: 2.8 us -> 2.35 us
    ppermute x1, waiting for transfers between devices: 5.67 us -> 1.04 us  [on_device(): got_b = lax.ppermute(lon_b, 'lon', partners('lon', 1, True))]
    ppermute x0 -> x1, starting transfers between devices: none -> 3.89 us  [on_device(): got_early = lax.ppermute(early, 'lon', partners('lon', 1, True))]
    unnamed x5 -> x6, local copies, waits for them, and re-layouts: 2.69 us -> 0.01 us
    pallas_call x1 -> x2, Pallas kernels: 2.69 us -> 3.16 us  [the longest x1 3.12 us: on_device(): pl.pallas_call(near_kernel, out_shape=(shape(SLABS, OWN, out_ch, dtype=F3...]
    ppermute x1, starting transfers between devices: 3.9 us -> 4.36 us  [on_device(): got_b = lax.ppermute(lon_b, 'lon', partners('lon', 1, True))]
    all_gather x1, blocking collectives: 2.8 us -> 2.35 us  [on_device(): both = lax.all_gather(lon_a, 'lon', axis_index_groups=chips)]
  transfers between devices with their start and end apart: 4 -> 5, of which waited for: 1 -> 1; matrix products, arithmetic and copies ran while one was open for 7% -> 0% of each run, Pallas kernels for 7% -> 9%
where the time goes in v6:
time: 38 us; the launch traced here: 37.3 us
  starting transfers between devices  24.6 us (65%)
  Pallas kernels  9.14 us (24%)
  blocking collectives  2.35 us (6%)
  waiting for transfers between devices  1.05 us (3%)
    ppermute x1, starting transfers between devices, on_device(): got_up = lax.ppermute(to_north, 'lat', [(i, j) for i, j in swaps if i > j])  8.38 us
    ppermute x1, starting transfers between devices, on_device(): got_a = lax.ppermute(to_partner, 'lat', partners('lat', 0, False))  6.71 us
    ppermute x1, starting transfers between devices, on_device(): got_b = lax.ppermute(lon_b, 'lon', partners('lon', 1, True))  4.36 us
    ppermute x1, starting transfers between devices, on_device(): got_early = lax.ppermute(early, 'lon', partners('lon', 1, True))  3.89 us
    pallas_call x1, Pallas kernels, on_device(): pl.pallas_call(far_kernel, out_shape=shape(ROWS, COLS, out_ch, dtype=F32)...  3.67 us
    pallas_call x1, Pallas kernels, on_device(): pl.pallas_call(near_kernel, out_shape=(shape(SLABS, OWN, out_ch, dtype=F3...  3.12 us
    all_gather x1, blocking collectives, on_device(): both = lax.all_gather(lon_a, 'lon', axis_index_groups=chips)  2.35 us
    pallas_call x1, Pallas kernels, on_device(): pl.pallas_call(down_kernel, out_shape=(shape(SLABS, OWN, chans), shape(CO...  2.18 us
  transfers between devices with their start and end apart: 5, of which 1 were waited for; matrix products, arithmetic and copies ran while one was open for 0% of the time, Pallas kernels for 9%

profile of v6, /device:TPU:57, one launch (start us, length us, event | category | flops | bytes accessed | tf_op | source)
XLA Modules:
  0.0 37.3 jit_solution(17613616548235115255)
XLA Ops:
  0.0 0.0 copy-start.1
  0.0 0.0 copy-start.2
  0.0 0.0 copy-start
  0.0 2.2 %down.1 = (bf16[4,128,256]{2,1,0:T(8,128)(2,1)S(1)}, bf16[16,256]{1,0:T(8,128)(2,1)S(1)}, bf16[48,256]{1,0:T(8,128)(2,1)S(1)}, f32[4,128,128]{2,1,0:T(8,128)S(1)...) custom-call(f32[64,32,256]{2,1,0:T(8,128)} %f_hbm.1, ...), custom_call_target="tpu_custom_call" | custom-call | tf_op jit(solution)/shard_map/down/pallas_call | solution.py:410
  2.2 1.3 %collective-permute-start = (bf16[224,256]{1,0:T(8,128)(2,1)S(1)}, bf16[224,256]{1,0:T(8,128)(2,1)S(1)}, u32[]{:S(2)}, u32[]{:S(2)}) collective-permute-start(bf16[224,256]{1,0:T(8,128)(2,1)S(1)} %get-tuple-element.22), channel_id=1, source_target_pairs={{32,64},{96,128},{160,192},{224,256},{288,320},{352,384},{416,448}... | collective-permute-start | bytes 344072 | tf_op jit(solution)/shard_map/ppermute | solution.py:439
  3.5 6.7 %collective-permute-start.1 = (bf16[224,256]{1,0:T(8,128)(2,1)S(1)}, bf16[224,256]{1,0:T(8,128)(2,1)S(1)}, u32[]{:S(2)}, u32[]{:S(2)}) collective-permute-start(bf16[224,256]{1,0:T(8,128)(2,1)S(1)} %get-tuple-element.23), channel_id=1, source_target_pairs={{0,32},{32,0},{64,96},{96,64},{128,160},{160,128},{192,224},{224,1... | collective-permute-start | bytes 344072 | tf_op jit(solution)/shard_map/ppermute | solution.py:440
  10.2 8.4 %collective-permute-start.2 = (bf16[224,256]{1,0:T(8,128)(2,1)S(1)}, bf16[224,256]{1,0:T(8,128)(2,1)S(1)}, u32[]{:S(2)}, u32[]{:S(2)}) collective-permute-start(bf16[224,256]{1,0:T(8,128)(2,1)S(1)} %get-tuple-element.24), channel_id=1, source_target_pairs={{64,32},{128,96},{192,160},{256,224},{320,288},{384,352},{448,416}... | collective-permute-start | bytes 344072 | tf_op jit(solution)/shard_map/ppermute | solution.py:441
  18.6 3.9 %collective-permute-start.3 = (bf16[368,256]{1,0:T(8,128)(2,1)S(1)}, bf16[368,256]{1,0:T(8,128)(2,1)S(1)}, u32[]{:S(2)}, u32[]{:S(2)}) collective-permute-start(bf16[368,256]{1,0:T(8,128)(2,1)S(1)} %early.1), channel_id=1, source_target_pairs={{1,2},{2,1},{3,4},{4,3},{5,6},{6,5},{7,8},{8,7},{9,10},{10,9},{11,... | collective-permute-start | bytes 565256 | tf_op jit(solution)/shard_map/ppermute | solution.py:453
  22.5 0.0 copy-done.1
  22.6 0.0 copy-done.2
  22.6 0.0 collective-permute-done.down_ref
  22.6 0.0 collective-permute-done.1.ra_ref
  22.6 0.0 collective-permute-done.2.up_ref
  22.6 0.1 band.1
  22.8 4.4 %collective-permute-start.4 = (bf16[368,256]{1,0:T(8,128)(2,1)S(1)}, bf16[368,256]{1,0:T(8,128)(2,1)S(1)}, u32[]{:S(2)}, u32[]{:S(2)}) collective-permute-start(bf16[368,256]{1,0:T(8,128)(2,1)S(1)} %get-tuple-element.27), channel_id=1, source_target_pairs={{1,2},{2,1},{3,4},{4,3},{5,6},{6,5},{7,8},{8,7},{9,10},{10,9},{11,... | collective-permute-start | bytes 565256 | tf_op jit(solution)/shard_map/ppermute | solution.py:475
  27.1 2.3 %all-gather = bf16[1472,256]{1,0:T(8,128)(2,1)S(1)} all-gather(bf16[736,256]{1,0:T(8,128)(2,1)S(1)} %get-tuple-element.28), channel_id=2, replica_groups={{0,1},{2,3},{4,5},{6,7},{8,9},{10,11},{12,13},{14,15},{16,17},{18,19},{..., dimensions={0}, use_global_device_ids=true | all-gather | bytes 1130496 | tf_op jit(solution)/shard_map/all_gather | solution.py:478
  29.5 0.0 copy-done
  29.5 3.1 %near_half.1 = (f32[4,128,300]{2,1,0:T(8,128)S(1)}, bf16[3,3,256,256]{3,2,1,0:T(8,128)(2,1)S(1)}, bf16[3,256,256]{2,1,0:T(8,128)(2,1)S(1)}) custom-call(bf16[4,224,256]{2,1,0:T(8,128)(2,1)S(1)} %get-tuple-element.25.band_ref, bf16[64,256]{1,0:T(8,128)(2,1)S(1)} %get-tuple-element.26.col_ref, bf16[2,736,256]{2,1,0:T(8,128)(2,1)S(1)} %bitcast.4, ...), custom_call_target="tpu_custom_call" | custom-call | flops 1476403200 | bytes 4194304 | tf_op jit(solution)/shard_map/near_half/pallas_call | solution.py:493
  32.6 0.0 collective-permute-done.3.early_ref
  32.6 1.0 %collective-permute-done.4.late_ref = bf16[368,256]{1,0:T(8,128)(2,1)S(1)} collective-permute-done((bf16[368,256]{1,0:T(8,128)(2,1)S(1)}, bf16[368,256]{1,0:T(8,128)(2,1)S(1)}, u32[]{:S(2)}, u32[]{:S(2)}) %collective-permute-start.4) | collective-permute-done | bytes 188448 | tf_op jit(solution)/shard_map/ppermute | solution.py:475
  33.7 3.7 %far_half.1 = f32[32,16,300]{2,1,0:T(8,128)} custom-call(bf16[4,224,256]{2,1,0:T(8,128)(2,1)S(1)} %get-tuple-element.25.band_ref, bf16[64,256]{1,0:T(8,128)(2,1)S(1)} %get-tuple-element.26.col_ref, bf16[368,256]{1,0:T(8,128)(2,1)S(1)} %collective-permute-done.3.early_ref, bf16[368,256]{1,0:T(8,128)(2,1)S(1)} %collective-permute-done.4.late_ref, ...), custom_call_target="tpu_custom_call" | custom-call | flops 1476403200 | bytes 4194304 | tf_op jit(solution)/shard_map/far_half/pallas_call | solution.py:508
  (3 shorter events, 0.0 us)
Async XLA Ops:
  0.0 22.5 %copy-start.1 = (f32[300]{0:T(512)S(1)}, f32[300]{0:T(512)}, u32[]{:S(2)}) copy-start(f32[300]{0:T(512)} %param.13) | copy-start | bytes 3604
  0.0 22.6 %copy-start.2 = (f32[300]{0:T(512)S(1)}, f32[300]{0:T(512)}, u32[]{:S(2)}) copy-start(f32[300]{0:T(512)} %param.15) | copy-start | bytes 3604
  0.0 29.5 %copy-start = (bf16[3,3,256,300]{2,3,1,0:T(8,128)(2,1)S(1)}, bf16[3,3,256,300]{2,3,1,0:T(8,128)(2,1)}, u32[]{:S(2)}) copy-start(bf16[3,3,256,300]{2,3,1,0:T(8,128)(2,1)} %param.12) | copy-start | bytes 4147204
  2.2 20.4 %collective-permute-start = (bf16[224,256]{1,0:T(8,128)(2,1)S(1)}, bf16[224,256]{1,0:T(8,128)(2,1)S(1)}, u32[]{:S(2)}, u32[]{:S(2)}) collective-permute-start(bf16[224,256]{1,0:T(8,128)(2,1)S(1)} %get-tuple-element.22), channel_id=1, source_target_pairs={{32,64},{96,128},{160,192},{224,256},{288,320},{352,384},{416,448}... | collective-permute-start | bytes 344072 | tf_op jit(solution)/shard_map/ppermute | solution.py:439
  3.5 19.1 %collective-permute-start.1 = (bf16[224,256]{1,0:T(8,128)(2,1)S(1)}, bf16[224,256]{1,0:T(8,128)(2,1)S(1)}, u32[]{:S(2)}, u32[]{:S(2)}) collective-permute-start(bf16[224,256]{1,0:T(8,128)(2,1)S(1)} %get-tuple-element.23), channel_id=1, source_target_pairs={{0,32},{32,0},{64,96},{96,64},{128,160},{160,128},{192,224},{224,1... | collective-permute-start | bytes 344072 | tf_op jit(solution)/shard_map/ppermute | solution.py:440
  10.2 12.4 %collective-permute-start.2 = (bf16[224,256]{1,0:T(8,128)(2,1)S(1)}, bf16[224,256]{1,0:T(8,128)(2,1)S(1)}, u32[]{:S(2)}, u32[]{:S(2)}) collective-permute-start(bf16[224,256]{1,0:T(8,128)(2,1)S(1)} %get-tuple-element.24), channel_id=1, source_target_pairs={{64,32},{128,96},{192,160},{256,224},{320,288},{384,352},{448,416}... | collective-permute-start | bytes 344072 | tf_op jit(solution)/shard_map/ppermute | solution.py:441
  18.6 14.0 %collective-permute-start.3 = (bf16[368,256]{1,0:T(8,128)(2,1)S(1)}, bf16[368,256]{1,0:T(8,128)(2,1)S(1)}, u32[]{:S(2)}, u32[]{:S(2)}) collective-permute-start(bf16[368,256]{1,0:T(8,128)(2,1)S(1)} %early.1), channel_id=1, source_target_pairs={{1,2},{2,1},{3,4},{4,3},{5,6},{6,5},{7,8},{8,7},{9,10},{10,9},{11,... | collective-permute-start | bytes 565256 | tf_op jit(solution)/shard_map/ppermute | solution.py:453
  22.8 10.9 %collective-permute-start.4 = (bf16[368,256]{1,0:T(8,128)(2,1)S(1)}, bf16[368,256]{1,0:T(8,128)(2,1)S(1)}, u32[]{:S(2)}, u32[]{:S(2)}) collective-permute-start(bf16[368,256]{1,0:T(8,128)(2,1)S(1)} %get-tuple-element.27), channel_id=1, source_target_pairs={{1,2},{2,1},{3,4},{4,3},{5,6},{6,5},{7,8},{8,7},{9,10},{10,9},{11,... | collective-permute-start | bytes 565256 | tf_op jit(solution)/shard_map/ppermute | solution.py:475

commit v7 on v6

--- a/solution.py
+++ b/solution.py
@@ -22,7 +22,7 @@
 LANES = 128
 MAIN = 256
 PAD = 64
-CHUNKS = 4
+CHUNKS = 2
 MASKED = 2.0**100
 LIMIT = 2.0**90
 F32 = jnp.float32
@@ -228,7 +228,7 @@
 
 def half_sums(
     side_west, band_ref, col_ref, from_west, from_east, w1_ref, w1_rest, b1_ref, w2_ref, load, sums, emit,
-    west_col, joined, ext, hidden, hidden_rest, w2_rest,
+    west_col, joined, ext, hidden, hidden_rest, w2_rest, gather,
 ):
     lat = lax.axis_index("lat")
     last = lax.axis_size("lat") - 1
@@ -291,10 +291,11 @@
             ].astype(BF16)
 
     load.wait()
-    w2_rest[...] = jnp.zeros_like(w2_rest)
-    for a in range(3):
-        for b in range(3):
-            w2_rest[b, PAD * a : PAD * a + rest] = w2_ref[a, b, MAIN:]
+    if gather:
+        w2_rest[...] = jnp.zeros_like(w2_rest)
+        for a in range(3):
+            for b in range(3):
+                w2_rest[b, PAD * a : PAD * a + rest] = w2_ref[a, b, MAIN:]
 
     def second(first_slab):
         for k in range(SLABS):
@@ -324,8 +325,8 @@
 
 def near_kernel(
     band_ref, col_ref, both_ref, stored_ref, b1_ref, w2_hbm, b2_ref,
-    sums_ref, w1_ref, w1_rest,
-    w2_ref, w2_sem, west_col, joined, ext, hidden, hidden_rest, w2_rest, stack,
+    sums_ref, w1_ref, w1_rest, w2_rest,
+    w2_ref, w2_sem, west_col, joined, ext, hidden, hidden_rest, stack,
 ):
     load = pltpu.make_async_copy(w2_hbm, w2_ref, w2_sem)
     load.start()
@@ -344,14 +345,14 @@
     odd = lax.rem(lax.axis_index("lon"), 2) == 1
     half_sums(
         odd, band_ref, col_ref, both_ref.at[0], both_ref.at[1], w1_ref, w1_rest, b1_ref, w2_ref, load, [start] * SLABS, emit,
-        west_col, joined, ext, hidden, hidden_rest, w2_rest,
+        west_col, joined, ext, hidden, hidden_rest, w2_rest, True,
     )
 
 
 def far_kernel(
-    band_ref, col_ref, early_ref, late_ref, w1_ref, w1_rest, b1_ref, w2_hbm, near_ref, keep_ref,
+    band_ref, col_ref, early_ref, late_ref, w1_ref, w1_rest, b1_ref, w2_hbm, near_ref, keep_ref, w2_rest,
     out_ref,
-    w2_ref, w2_sem, west_col, joined, ext, hidden, hidden_rest, w2_rest, far_ref, far_col,
+    w2_ref, w2_sem, west_col, joined, ext, hidden, hidden_rest, far_ref, far_col,
 ):
     load = pltpu.make_async_copy(w2_hbm, w2_ref, w2_sem)
     load.start()
@@ -377,7 +378,7 @@
     even = lax.rem(lax.axis_index("lon"), 2) == 0
     half_sums(
         even, band_ref, col_ref, far_ref, far_ref, w1_ref, w1_rest, b1_ref, w2_ref, load, near_ref, emit,
-        west_col, joined, ext, hidden, hidden_rest, w2_rest,
+        west_col, joined, ext, hidden, hidden_rest, w2_rest, False,
     )
 
 
@@ -485,20 +486,20 @@
         pltpu.VMEM((2 * HALO_SLABS, EXT, chans), BF16),
         pltpu.VMEM((SIDE, HID, MAIN), BF16),
         pltpu.VMEM((SIDE, OWN, 3 * PAD), BF16),
-        pltpu.VMEM((3, 3 * PAD, out_ch), BF16),
     ]
     w_two, b_one = in_hbm(w_two), b_one[None]
     flops = 2 * SIDE * HID * 9 * chans * out_ch + 2 * 6 * OWN * 3 * out_ch * out_ch
     cost = pl.CostEstimate(flops=flops, bytes_accessed=4 << 20, transcendentals=SIDE * HID * out_ch)
-    near, w1_main, w1_rest = pl.pallas_call(
+    near, w1_main, w1_rest, w2_rest = pl.pallas_call(
         near_kernel,
         out_shape=(
             shape(SLABS, OWN, out_ch, dtype=F32),
             shape(3, 3, chans, MAIN),
             shape(3, chans, MAIN),
+            shape(3, 3 * PAD, out_ch),
         ),
         in_specs=[vmem] * 5 + [hbm, vmem],
-        out_specs=[vmem] * 3,
+        out_specs=[vmem] * 4,
         scratch_shapes=scratch + [pltpu.VMEM((3, MAIN, chans), BF16)],
         compiler_params=pltpu.CompilerParams(vmem_limit_bytes=14 << 20),
         cost_estimate=cost,
@@ -508,14 +509,14 @@
     return pl.pallas_call(
         far_kernel,
         out_shape=shape(ROWS, COLS, out_ch, dtype=F32),
-        in_specs=[vmem] * 7 + [hbm, vmem, vmem],
+        in_specs=[vmem] * 7 + [hbm, vmem, vmem, vmem],
         out_specs=vmem,
         scratch_shapes=scratch
         + [pltpu.VMEM((lon_rows, chans), BF16), pltpu.VMEM((64, chans), F32)],
         compiler_params=pltpu.CompilerParams(vmem_limit_bytes=14 << 20),
         cost_estimate=cost,
         name="far_half",
-    )(band, col, got_early, got_b, w1_main, w1_rest, b_one, w_two, near, keep)
+    )(band, col, got_early, got_b, w1_main, w1_rest, b_one, w_two, near, keep, w2_rest)
 
 
 def solution(mesh):

time: 38 us -> 37.9 us (level)
  no operation moved by 1% of the time
where the time goes in v7:
time: 37.9 us; the launch traced here: 37.1 us
  starting transfers between devices  24.6 us (65%)
  Pallas kernels  8.95 us (24%)
  blocking collectives  2.35 us (6%)
  waiting for transfers between devices  1.04 us (3%)
    ppermute x1, starting transfers between devices, on_device(): got_up = lax.ppermute(to_north, 'lat', [(i, j) for i, j in swaps if i > j])  8.38 us
    ppermute x1, starting transfers between devices, on_device(): got_a = lax.ppermute(to_partner, 'lat', partners('lat', 0, False))  6.71 us
    ppermute x1, starting transfers between devices, on_device(): got_b = lax.ppermute(lon_b, 'lon', partners('lon', 1, True))  4.36 us
    ppermute x1, starting transfers between devices, on_device(): got_early = lax.ppermute(early, 'lon', partners('lon', 1, True))  3.89 us
    pallas_call x1, Pallas kernels, on_device(): pl.pallas_call(far_kernel, out_shape=shape(ROWS, COLS, out_ch, dtype=F32)...  3.6 us
    pallas_call x1, Pallas kernels, on_device(): pl.pallas_call(near_kernel, out_shape=(shape(SLABS, OWN, out_ch, dtype=F3...  3.14 us
    all_gather x1, blocking collectives, on_device(): both = lax.all_gather(lon_a, 'lon', axis_index_groups=chips)  2.35 us
    pallas_call x1, Pallas kernels, on_device(): pl.pallas_call(down_kernel, out_shape=(shape(SLABS, OWN, chans), shape(CO...  2.05 us
  transfers between devices with their start and end apart: 5, of which 1 were waited for; matrix products, arithmetic and copies ran while one was open for 0% of the time, Pallas kernels for 9%

profile of v7, /device:TPU:57, one launch (start us, length us, event | category | flops | bytes accessed | tf_op | source)
XLA Modules:
  0.0 37.1 jit_solution(10758490810380420104)
XLA Ops:
  0.0 0.0 copy-start.1
  0.0 0.0 copy-start.2
  0.0 0.0 copy-start
  0.0 2.0 %down.1 = (bf16[4,128,256]{2,1,0:T(8,128)(2,1)S(1)}, bf16[16,256]{1,0:T(8,128)(2,1)S(1)}, bf16[48,256]{1,0:T(8,128)(2,1)S(1)}, f32[4,128,128]{2,1,0:T(8,128)S(1)...) custom-call(f32[64,32,256]{2,1,0:T(8,128)} %f_hbm.1, ...), custom_call_target="tpu_custom_call" | custom-call | tf_op jit(solution)/shard_map/down/pallas_call | solution.py:411
  2.1 1.3 %collective-permute-start = (bf16[224,256]{1,0:T(8,128)(2,1)S(1)}, bf16[224,256]{1,0:T(8,128)(2,1)S(1)}, u32[]{:S(2)}, u32[]{:S(2)}) collective-permute-start(bf16[224,256]{1,0:T(8,128)(2,1)S(1)} %get-tuple-element.23), channel_id=1, source_target_pairs={{32,64},{96,128},{160,192},{224,256},{288,320},{352,384},{416,448}... | collective-permute-start | bytes 344072 | tf_op jit(solution)/shard_map/ppermute | solution.py:440
  3.4 6.7 %collective-permute-start.1 = (bf16[224,256]{1,0:T(8,128)(2,1)S(1)}, bf16[224,256]{1,0:T(8,128)(2,1)S(1)}, u32[]{:S(2)}, u32[]{:S(2)}) collective-permute-start(bf16[224,256]{1,0:T(8,128)(2,1)S(1)} %get-tuple-element.24), channel_id=1, source_target_pairs={{0,32},{32,0},{64,96},{96,64},{128,160},{160,128},{192,224},{224,1... | collective-permute-start | bytes 344072 | tf_op jit(solution)/shard_map/ppermute | solution.py:441
  10.1 8.4 %collective-permute-start.2 = (bf16[224,256]{1,0:T(8,128)(2,1)S(1)}, bf16[224,256]{1,0:T(8,128)(2,1)S(1)}, u32[]{:S(2)}, u32[]{:S(2)}) collective-permute-start(bf16[224,256]{1,0:T(8,128)(2,1)S(1)} %get-tuple-element.25), channel_id=1, source_target_pairs={{64,32},{128,96},{192,160},{256,224},{320,288},{384,352},{448,416}... | collective-permute-start | bytes 344072 | tf_op jit(solution)/shard_map/ppermute | solution.py:442
  18.5 3.9 %collective-permute-start.3 = (bf16[368,256]{1,0:T(8,128)(2,1)S(1)}, bf16[368,256]{1,0:T(8,128)(2,1)S(1)}, u32[]{:S(2)}, u32[]{:S(2)}) collective-permute-start(bf16[368,256]{1,0:T(8,128)(2,1)S(1)} %early.1), channel_id=1, source_target_pairs={{1,2},{2,1},{3,4},{4,3},{5,6},{6,5},{7,8},{8,7},{9,10},{10,9},{11,... | collective-permute-start | bytes 565256 | tf_op jit(solution)/shard_map/ppermute | solution.py:454
  22.4 0.0 copy-done.1
  22.4 0.0 copy-done.2
  22.5 0.0 collective-permute-done.down_ref
  22.5 0.0 collective-permute-done.1.ra_ref
  22.5 0.0 collective-permute-done.2.up_ref
  22.5 0.1 band.1
  22.6 4.4 %collective-permute-start.4 = (bf16[368,256]{1,0:T(8,128)(2,1)S(1)}, bf16[368,256]{1,0:T(8,128)(2,1)S(1)}, u32[]{:S(2)}, u32[]{:S(2)}) collective-permute-start(bf16[368,256]{1,0:T(8,128)(2,1)S(1)} %get-tuple-element.28), channel_id=1, source_target_pairs={{1,2},{2,1},{3,4},{4,3},{5,6},{6,5},{7,8},{8,7},{9,10},{10,9},{11,... | collective-permute-start | bytes 565256 | tf_op jit(solution)/shard_map/ppermute | solution.py:476
  27.0 2.3 %all-gather = bf16[1472,256]{1,0:T(8,128)(2,1)S(1)} all-gather(bf16[736,256]{1,0:T(8,128)(2,1)S(1)} %get-tuple-element.29), channel_id=2, replica_groups={{0,1},{2,3},{4,5},{6,7},{8,9},{10,11},{12,13},{14,15},{16,17},{18,19},{..., dimensions={0}, use_global_device_ids=true | all-gather | bytes 1130496 | tf_op jit(solution)/shard_map/all_gather | solution.py:479
  29.4 0.0 copy-done
  29.4 3.1 %near_half.1 = (f32[4,128,300]{2,1,0:T(8,128)S(1)}, bf16[3,3,256,256]{3,2,1,0:T(8,128)(2,1)S(1)}, bf16[3,256,256]{2,1,0:T(8,128)(2,1)S(1)}, bf16[3,192,300]{2,1,0:T(8,128)(2,1)S(1)}) custom-call(bf16[4,224,256]{2,1,0:T(8,128)(2,1)S(1)} %get-tuple-element.26.band_ref, bf16[64,256]{1,0:T(8,128)(2,1)S(1)} %get-tuple-element.27.col_ref, ...), custom_call_target="tpu_custom_call" | custom-call | flops 1476403200 | bytes 4194304 | tf_op jit(solution)/shard_map/near_half/pallas_call | solution.py:493
  32.5 0.0 collective-permute-done.3.early_ref
  32.5 1.0 %collective-permute-done.4.late_ref = bf16[368,256]{1,0:T(8,128)(2,1)S(1)} collective-permute-done((bf16[368,256]{1,0:T(8,128)(2,1)S(1)}, bf16[368,256]{1,0:T(8,128)(2,1)S(1)}, u32[]{:S(2)}, u32[]{:S(2)}) %collective-permute-start.4) | collective-permute-done | bytes 188448 | tf_op jit(solution)/shard_map/ppermute | solution.py:476
  33.5 3.6 %far_half.1 = f32[32,16,300]{2,1,0:T(8,128)} custom-call(bf16[4,224,256]{2,1,0:T(8,128)(2,1)S(1)} %get-tuple-element.26.band_ref, bf16[64,256]{1,0:T(8,128)(2,1)S(1)} %get-tuple-element.27.col_ref, bf16[368,256]{1,0:T(8,128)(2,1)S(1)} %collective-permute-done.3.early_ref, bf16[368,256]{1,0:T(8,128)(2,1)S(1)} %collective-permute-done.4.late_ref, ...), custom_call_target="tpu_custom_call" | custom-call | flops 1476403200 | bytes 4194304 | tf_op jit(solution)/shard_map/far_half/pallas_call | solution.py:509
  (3 shorter events, 0.0 us)
Async XLA Ops:
  0.0 22.4 %copy-start.1 = (f32[300]{0:T(512)S(1)}, f32[300]{0:T(512)}, u32[]{:S(2)}) copy-start(f32[300]{0:T(512)} %param.13) | copy-start | bytes 3604
  0.0 22.4 %copy-start.2 = (f32[300]{0:T(512)S(1)}, f32[300]{0:T(512)}, u32[]{:S(2)}) copy-start(f32[300]{0:T(512)} %param.15) | copy-start | bytes 3604
  0.0 29.4 %copy-start = (bf16[3,3,256,300]{2,3,1,0:T(8,128)(2,1)S(1)}, bf16[3,3,256,300]{2,3,1,0:T(8,128)(2,1)}, u32[]{:S(2)}) copy-start(bf16[3,3,256,300]{2,3,1,0:T(8,128)(2,1)} %param.12) | copy-start | bytes 4147204
  2.1 20.4 %collective-permute-start = (bf16[224,256]{1,0:T(8,128)(2,1)S(1)}, bf16[224,256]{1,0:T(8,128)(2,1)S(1)}, u32[]{:S(2)}, u32[]{:S(2)}) collective-permute-start(bf16[224,256]{1,0:T(8,128)(2,1)S(1)} %get-tuple-element.23), channel_id=1, source_target_pairs={{32,64},{96,128},{160,192},{224,256},{288,320},{352,384},{416,448}... | collective-permute-start | bytes 344072 | tf_op jit(solution)/shard_map/ppermute | solution.py:440
  3.4 19.1 %collective-permute-start.1 = (bf16[224,256]{1,0:T(8,128)(2,1)S(1)}, bf16[224,256]{1,0:T(8,128)(2,1)S(1)}, u32[]{:S(2)}, u32[]{:S(2)}) collective-permute-start(bf16[224,256]{1,0:T(8,128)(2,1)S(1)} %get-tuple-element.24), channel_id=1, source_target_pairs={{0,32},{32,0},{64,96},{96,64},{128,160},{160,128},{192,224},{224,1... | collective-permute-start | bytes 344072 | tf_op jit(solution)/shard_map/ppermute | solution.py:441
  10.1 12.4 %collective-permute-start.2 = (bf16[224,256]{1,0:T(8,128)(2,1)S(1)}, bf16[224,256]{1,0:T(8,128)(2,1)S(1)}, u32[]{:S(2)}, u32[]{:S(2)}) collective-permute-start(bf16[224,256]{1,0:T(8,128)(2,1)S(1)} %get-tuple-element.25), channel_id=1, source_target_pairs={{64,32},{128,96},{192,160},{256,224},{320,288},{384,352},{448,416}... | collective-permute-start | bytes 344072 | tf_op jit(solution)/shard_map/ppermute | solution.py:442
  18.5 14.0 %collective-permute-start.3 = (bf16[368,256]{1,0:T(8,128)(2,1)S(1)}, bf16[368,256]{1,0:T(8,128)(2,1)S(1)}, u32[]{:S(2)}, u32[]{:S(2)}) collective-permute-start(bf16[368,256]{1,0:T(8,128)(2,1)S(1)} %early.1), channel_id=1, source_target_pairs={{1,2},{2,1},{3,4},{4,3},{5,6},{6,5},{7,8},{8,7},{9,10},{10,9},{11,... | collective-permute-start | bytes 565256 | tf_op jit(solution)/shard_map/ppermute | solution.py:454
  22.6 10.9 %collective-permute-start.4 = (bf16[368,256]{1,0:T(8,128)(2,1)S(1)}, bf16[368,256]{1,0:T(8,128)(2,1)S(1)}, u32[]{:S(2)}, u32[]{:S(2)}) collective-permute-start(bf16[368,256]{1,0:T(8,128)(2,1)S(1)} %get-tuple-element.28), channel_id=1, source_target_pairs={{1,2},{2,1},{3,4},{4,3},{5,6},{6,5},{7,8},{8,7},{9,10},{10,9},{11,... | collective-permute-start | bytes 565256 | tf_op jit(solution)/shard_map/ppermute | solution.py:476
